TPU v7x, 128 devices: a whole 4x4x4 slice. The times are simulated.
128 devices in a mesh: vel: 32 (over x_hi, y, z), space: 4 (over x_lo, core).
Axes of the slice: x: 4 (x_hi: 2, x_lo: 2; x = x_hi * 2 + x_lo), y: 4, z: 4, core: 2. Of those that a mesh axis runs over, the one named last changes fastest.
Arguments:
- dist: float32 [4096, 32, 1024], P('vel', 'space'), may hold values from -6 to 6
- vel_index: int32 [3, 4096], P(None, 'vel'), may hold values from 0 to 15, as said below
- relax: float32 [32, 1024], P('space'), may hold values from 0.05 to 0.9
- wall_mask: int32 [32, 1024], P('space'), may hold values 0 or 1
- macro_inverse: float32 [13, 13], replicated, may hold values from -1.5 to 1.5
Outputs:
- dist_out: float32 [4096, 32, 1024], P('vel', 'space')
- macro_fields: float32 [13, 32, 1024], P(None, 'space', 'vel')
- change_norm: float32 [2], replicated
Inputs may be any that keep to these rules, and one draw needn't show every extreme that they name: `vel_index`: each point of the velocity grid of 4096 points appears in exactly one column.
All inputs are finite; a program needn't handle non-finite values. No bound on the sum of `wall_mask` on one device may be relied on, other than what follows from the above.
Results may differ from a plain program's by a relative error of at most 0.0003.
Values sent between devices are 32-bit elements; how exact they have to be, the bound alone decides.
A program may use at most 128 MiB of HBM per device.

v0:
```python
import math

import jax
import jax.numpy as jnp
from jax import lax
from jax.sharding import PartitionSpec as P

NVX = 16
NY = 64
NZ = 16
MOM = 13
SWEEPS = 3
ITERS = 2


speed_range = 4.0
time_step = 0.08
coupling = 0.5


def with_halo(shard, sides, width):
    for axis, dim in sides:
        peers, length = (lax.axis_size(axis), shard.shape[dim])
        up = [(i, (i + 1) % peers) for i in range(peers)]
        down = [(j, i) for i, j in up]
        last = lax.slice_in_dim(shard, length - width, length, axis=dim)
        first = lax.slice_in_dim(shard, 0, width, axis=dim)
        before = lax.ppermute(last, axis, up)
        after = lax.ppermute(first, axis, down)
        shard = jnp.concatenate([before, shard, after], axis=dim)
    return shard


def velocities(vel_index):
    return speed_range * (2.0 * vel_index.astype(jnp.float32) + 1.0 - NVX) / NVX


def bases(velocity):
    cxv, cyv, czv = (velocity[0], velocity[1], velocity[2])
    square = cxv * cxv + cyv * cyv + czv * czv
    weights = (2.0 * speed_range / NVX) ** 3 * math.pi ** (-1.5) * jnp.exp(-square)
    heat = square - 2.5
    functions = jnp.stack(
        [
            jnp.ones_like(cxv),
            cxv,
            cyv,
            czv,
            2.0 * square / 3.0 - 1.0,
            2.0 * cxv * cyv,
            2.0 * cxv * czv,
            2.0 * cyv * czv,
            cxv * cxv - cyv * cyv,
            cyv * cyv - czv * czv,
            cxv * heat,
            cyv * heat,
            czv * heat,
        ],
        0,
    )
    moment_rows = functions * weights[None, :]
    factor = 4.0 / 15.0
    shakhov = jnp.stack(
        [
            jnp.ones_like(cxv),
            2.0 * cxv,
            2.0 * cyv,
            2.0 * czv,
            square - 1.5,
            factor * cxv * heat,
            factor * cyv * heat,
            factor * czv * heat,
        ],
        1,
    )
    walls = jnp.stack([jnp.ones_like(cxv), square - 1.5], 1)
    return (moment_rows, shakhov, walls)


def upwind_local(block, speed, axis):
    lower = jnp.roll(block, 1, axis)
    higher = jnp.roll(block, -1, axis)
    return jnp.where(speed > 0, block - lower, higher - block)


def stream(dist, velocity):
    count, width, cells = dist.shape
    padded = with_halo(dist, (("space", 1),), 1)
    lower_x = padded[:, :-2]
    higher_x = padded[:, 2:]
    cxv = velocity[0][:, None, None]
    cyv = velocity[1][:, None, None, None]
    czv = velocity[2][:, None, None, None]
    along_x = jnp.where(cxv > 0, dist - lower_x, higher_x - dist)
    grid = dist.reshape(count, width, NY, NZ)
    across = cyv * upwind_local(grid, cyv, 2) + czv * upwind_local(grid, czv, 3)
    total = cxv * along_x + across.reshape(count, width, cells)
    return dist - time_step * total


def slab_sweep(field):
    padded = with_halo(field, (("space", 1),), 1)
    beside_all = padded[:, :-2] + padded[:, 2:]
    for axis in (2, 3):
        beside_all = beside_all + jnp.roll(field, 1, axis) + jnp.roll(field, -1, axis)
    return beside_all


def smooth(local, neighbours):
    rows, width, cells = local.shape
    source = local[1:5].reshape(4, width, cells // NZ, NZ)
    field = source
    for sweep in range(SWEEPS):
        field = (source + coupling * neighbours(field)) / (1.0 + 6.0 * coupling)
    return jnp.concatenate([local[0:1], field.reshape(4, width, cells), local[5:]], 0)


def shards(dist, vel_index, relax, wall_mask, macro_inverse):
    highest = lax.Precision.HIGHEST
    count, width, cells = dist.shape
    share = cells // lax.axis_size("vel")
    velocity = velocities(vel_index)
    moment_rows, shakhov, walls = bases(velocity)
    norms = []
    owned_block = None
    for step in range(ITERS):
        read = stream(dist, velocity)
        partial_moments = jnp.dot(
            moment_rows, read.reshape(count, width * cells), precision=highest
        ).reshape(MOM, width, cells)
        totals = lax.psum(partial_moments, "vel")
        local = jnp.einsum("kj,jxc->kxc", macro_inverse, totals, precision=highest)
        updated = smooth(local, slab_sweep)
        change = lax.psum(jnp.sum((updated - totals) ** 2), "space")
        fields = jnp.concatenate([updated[0:5], updated[10:13]], 0)
        owned_block = lax.dynamic_slice_in_dim(updated, lax.axis_index("vel") * share, share, 2)
        norms.append(jnp.sqrt(change))
        flat_fields = fields.reshape(8, width * cells)
        target = jnp.dot(shakhov, flat_fields, precision=highest).reshape(count, width, cells)
        wall_fields = jnp.stack([flat_fields[0], flat_fields[4]], 0)
        wall_value = jnp.dot(walls, wall_fields, precision=highest).reshape(count, width, cells)
        dist = jnp.where(wall_mask[None] > 0, wall_value, read + relax[None] * (target - read))
    return (dist, owned_block, jnp.stack(norms))


def solution(mesh):
    return jax.shard_map(
        shards,
        mesh=mesh,
        in_specs=(P("vel", "space", None), P(None, "vel"), P("space", None), P("space", None), P()),
        out_specs=(P("vel", "space", None), P(None, "space", "vel"), P()),
        check_vma=False,
    )
```

profile of v0, /device:TPU:1, one launch (start us, length us, event | category | flops | bytes accessed | tf_op | source)
XLA Modules:
  0.0 973.0 jit_solution(570978027934620654)
XLA Ops:
  7.2 4.6 copy.217
  11.9 2.0 copy-done.4
  14.9 2.6 collective-permute-start
  17.7 5.4 copy.208
  23.1 4.1 fusion.104
  29.1 4.1 pad_maximum_fusion.4
  33.2 4.2 pad_maximum_fusion.6
  37.4 5.3 copy.210
  42.8 5.4 copy.211
  48.2 5.4 copy.214
  53.6 5.3 copy.215
  59.1 13.7 %fusion.12 = f32[128,8,1024]{2,0,1:T(8,128)} fusion(f32[128,8,1024]{2,0,1:T(8,128)} %copy-done.4, f32[128,1,1024]{2,0,1:T(8,128)} %collective-permute-done.1, f32[128,1,1024]{2,0,1:T(8,128)S(1)} %collective-permute-done, f32[128,8,1024]{2,0,1:T(8,128)} %copy.215, f32[128,8,1024]{2,0,1:T(8,128)} %copy.214, f32[128,8,1024]{2,0,1:T(8,128)} %copy.211, ...), kind=kLoop, calls=%fused_computation.16 | loop fusion | flops 18874368 | bytes 26216320 | tf_op jit(solution)/shard_map/sub | solution.py:98
  72.8 5.3 copy.218
  78.1 6.5 fusion.16
  84.9 334.3 %all-reduce.5.cloned.1.call-done = f32[13,8,1024]{2,0,1:T(8,128)} async-done(((f32[13,8,1024]{2,0,1:T(8,128)}), f32[13,8,1024]{2,0,1:T(8,128)}) %all-reduce.5.cloned.1.call-update) | async-done | bytes 426000 | tf_op jit(solution)/shard_map/psum | solution.py:131
  419.2 1.6 convolution_bitcast_fusion.1
  422.3 21.9 %collective-permute-start.2 = (f32[4,1,64,16]{3,2,1,0:T(8,128)S(1)}, f32[4,1,64,16]{3,2,1,0:T(8,128)S(1)}, u32[]{:S(2)}, u32[]{:S(2)}) collective-permute-start(f32[4,1,64,16]{3,2,1,0:T(8,128)S(1)} %get-tuple-element.97), channel_id=1, source_target_pairs={{0,1},{1,2},{2,3},{3,0},{4,5},{5,6},{6,7},{7,4},{8,9},{9,10},{10,1... | collective-permute-start | bytes 49160 | tf_op jit(solution)/shard_map/ppermute | solution.py:28
  444.4 1.9 collective-permute-done.2
  446.2 3.0 collective-permute-done.3
  453.2 3.0 collective-permute-done.5
  460.2 2.9 collective-permute-done.7
  464.9 3.5 fusion.68
  468.5 5.7 bitcast_select_fusion
  474.2 5.3 copy.221
  479.5 4.1 fusion.99
  484.1 4.1 fusion.101
  488.7 2.3 fusion.102
  491.6 2.4 pad_maximum_fusion.8
  494.0 2.4 pad_maximum_fusion.9
  496.4 5.3 copy.222
  501.7 5.4 copy.223
  507.1 4.8 pad_maximum_fusion.10
  511.9 5.4 copy.224
  517.3 4.7 pad_maximum_fusion.11
  522.0 5.4 copy.225
  527.4 13.5 %fusion.5 = f32[128,8,1024]{2,0,1:T(8,128)} fusion(f32[128,8,1024]{2,0,1:T(8,128)} %bitcast_select_fusion, f32[128,1,1024]{2,0,1:T(8,128)S(1)} %collective-permute-done.9, f32[128,1,1024]{2,0,1:T(8,128)S(1)} %collective-permute-done.8, f32[128,8,1024]{2,0,1:T(8,128)} %copy.225, f32[128,8,1024]{2,0,1:T(8,128)} %copy.224, f32[128,8,1024]{2,0,1:T(8,128)} %copy.223, ...), kind=kLoop, calls=%fused_computation.7 | loop fusion | flops 18874368 | bytes 26216320 | tf_op jit(solution)/shard_map/sub | solution.py:98
  540.9 5.3 copy.226
  546.2 6.5 fusion.14
  554.3 330.8 %all-reduce.7.cloned.1.call-done = f32[13,8,1024]{2,0,1:T(8,128)} async-done(((f32[13,8,1024]{2,0,1:T(8,128)}), f32[13,8,1024]{2,0,1:T(8,128)}) %all-reduce.7.cloned.1.call-update) | async-done | bytes 426000 | tf_op jit(solution)/shard_map/psum | solution.py:131
  888.2 21.9 %collective-permute-start.10 = (f32[4,1,64,16]{3,2,1,0:T(8,128)S(1)}, f32[4,1,64,16]{3,2,1,0:T(8,128)S(1)}, u32[]{:S(2)}, u32[]{:S(2)}) collective-permute-start(f32[4,1,64,16]{3,2,1,0:T(8,128)S(1)} %get-tuple-element.67), channel_id=1, source_target_pairs={{0,1},{1,2},{2,3},{3,0},{4,5},{5,6},{6,7},{7,4},{8,9},{9,10},{10,1... | collective-permute-start | bytes 49160 | tf_op jit(solution)/shard_map/ppermute | solution.py:28
  912.1 3.0 collective-permute-done.11
  919.1 2.8 collective-permute-done.13
  926.0 2.7 collective-permute-done.15
  931.7 6.0 all-reduce.1
  940.0 8.2 fusion.72
  948.2 5.3 copy.229
  953.6 7.2 add_select_fusion
  960.8 4.4 copy.232
  (126 shorter events, 35.5 us)
Async XLA Ops:
  7.2 412.0 %copy-start = (f32[13,13]{1,0:T(8,128)S(1)}, f32[13,13]{1,0:T(8,128)}, u32[]{:S(2)}) copy-start(f32[13,13]{1,0:T(8,128)} %param.9) | copy-start | bytes 2032
  7.2 412.0 %all-reduce.5.cloned.1.call-start = ((), (), s32[]{:S(2)}) async-start(), calls=%async_computation | async-start | bytes 1048576 | tf_op jit(solution)/shard_map/psum | solution.py:131
  11.8 2.0 copy-start.4
  14.9 44.1 %collective-permute-start = (f32[128,1,1024]{2,0,1:T(8,128)}, f32[128,1,1024]{2,0,1:T(8,128)S(1)}, u32[]{:S(2)}, u32[]{:S(2)}) collective-permute-start(f32[128,1,1024]{2,0,1:T(8,128)} %get-tuple-element.37), channel_id=1, source_target_pairs={{0,1},{1,2},{2,3},{3,0},{4,5},{5,6},{6,7},{7,4},{8,9},{9,10},{10,1... | collective-permute-start | bytes 1572872 | tf_op jit(solution)/shard_map/ppermute | solution.py:28
  17.5 41.5 %collective-permute-start.1 = (f32[128,1,1024]{2,0,1:T(8,128)}, f32[128,1,1024]{2,0,1:T(8,128)}, u32[]{:S(2)}, u32[]{:S(2)}) collective-permute-start(f32[128,1,1024]{2,0,1:T(8,128)} %get-tuple-element.38), channel_id=1, source_target_pairs={{1,0},{2,1},{3,2},{0,3},{5,4},{6,5},{7,6},{4,7},{9,8},{10,9},{11,1... | collective-permute-start | bytes 1572872 | tf_op jit(solution)/shard_map/ppermute | solution.py:29
  23.1 4.6 copy-start.1
  27.7 1.4 copy-start.9
  78.1 6.8 copy-start.8
  84.6 800.5 %all-reduce.7.cloned.1.call-start = ((), (), s32[]{:S(2)}) async-start(), calls=%async_computation.1 | async-start | bytes 1048576 | tf_op jit(solution)/shard_map/psum | solution.py:131
  422.3 23.9 %collective-permute-start.2 = (f32[4,1,64,16]{3,2,1,0:T(8,128)S(1)}, f32[4,1,64,16]{3,2,1,0:T(8,128)S(1)}, u32[]{:S(2)}, u32[]{:S(2)}) collective-permute-start(f32[4,1,64,16]{3,2,1,0:T(8,128)S(1)} %get-tuple-element.97), channel_id=1, source_target_pairs={{0,1},{1,2},{2,3},{3,0},{4,5},{5,6},{6,7},{7,4},{8,9},{9,10},{10,1... | collective-permute-start | bytes 49160 | tf_op jit(solution)/shard_map/ppermute | solution.py:28
  444.3 4.9 collective-permute-start.3
  451.2 2.0 collective-permute-start.4
  451.3 4.9 collective-permute-start.5
  458.2 2.0 collective-permute-start.6
  458.3 4.9 collective-permute-start.7
  464.1 4.4 copy-start.7
  464.9 3.6 copy-start.3
  479.5 4.6 copy-start.2
  491.0 36.4 %collective-permute-start.8 = (f32[128,1,1024]{2,0,1:T(8,128)}, f32[128,1,1024]{2,0,1:T(8,128)S(1)}, u32[]{:S(2)}, u32[]{:S(2)}) collective-permute-start(f32[128,1,1024]{2,0,1:T(8,128)} %get-tuple-element.27), channel_id=1, source_target_pairs={{0,1},{1,2},{2,3},{3,0},{4,5},{5,6},{6,7},{7,4},{8,9},{9,10},{10,1... | collective-permute-start | bytes 1572872 | tf_op jit(solution)/shard_map/ppermute | solution.py:28
  491.0 36.4 %collective-permute-start.9 = (f32[128,1,1024]{2,0,1:T(8,128)}, f32[128,1,1024]{2,0,1:T(8,128)S(1)}, u32[]{:S(2)}, u32[]{:S(2)}) collective-permute-start(f32[128,1,1024]{2,0,1:T(8,128)} %get-tuple-element.28), channel_id=1, source_target_pairs={{1,0},{2,1},{3,2},{0,3},{5,4},{6,5},{7,6},{4,7},{9,8},{10,9},{11,1... | collective-permute-start | bytes 1572872 | tf_op jit(solution)/shard_map/ppermute | solution.py:29
  546.2 7.3 copy-start.5
  888.2 23.9 %collective-permute-start.10 = (f32[4,1,64,16]{3,2,1,0:T(8,128)S(1)}, f32[4,1,64,16]{3,2,1,0:T(8,128)S(1)}, u32[]{:S(2)}, u32[]{:S(2)}) collective-permute-start(f32[4,1,64,16]{3,2,1,0:T(8,128)S(1)} %get-tuple-element.67), channel_id=1, source_target_pairs={{0,1},{1,2},{2,3},{3,0},{4,5},{5,6},{6,7},{7,4},{8,9},{9,10},{10,1... | collective-permute-start | bytes 49160 | tf_op jit(solution)/shard_map/ppermute | solution.py:28
  910.2 4.9 collective-permute-start.11
  917.1 2.0 collective-permute-start.12
  917.2 4.7 collective-permute-start.13
  923.9 2.0 collective-permute-start.14
  924.0 4.6 collective-permute-start.15
  928.7 2.3 copy-start.6
Sparse Core Ops, SparseCore 0:
  84.7 334.4 all-reduce.4
  552.9 332.1 all-reduce.6
where the time goes:
time: 977 us; the launch traced here: 973 us
  waiting for transfers between devices  691 us (71%)
  local copies, waits for them, and re-layouts  110 us (11%)
  other arithmetic  57.9 us (6%)
  starting transfers between devices  50.5 us (5%)
  matrix products  40.9 us (4%)
  between operations  16.4 us (2%)
    psum x2, waiting for transfers between devices, shards(): totals = lax.psum(partial_moments, 'vel')  665 us
    ppermute x8, starting transfers between devices, with_halo(): before = lax.ppermute(last, axis, up)  46.8 us
    sub x2, other arithmetic, stream(): return dist - time_step * total  27.2 us
    concatenate x4, local copies, waits for them, and re-layouts, upwind_local(): higher = jnp.roll(block, -1, axis)  21.6 us
    concatenate x4, local copies, waits for them, and re-layouts, upwind_local(): lower = jnp.roll(block, 1, axis)  21.4 us
  transfers between devices with their start and end apart: 18, of which 14 were waited for; matrix products, arithmetic and copies ran while one was open for 8% of the time, Pallas kernels for 0%

commit v1 on v0

v1 whole, which is shorter than its diff:
```python
import functools
import math

import jax
import jax.numpy as jnp
import numpy as np
from jax import lax
from jax.experimental import pallas as pl
from jax.experimental.pallas import tpu as pltpu
from jax.sharding import PartitionSpec as P

NVX = 16
NZ = 16
MOM = 13
SWEEPS = 3
speed_range = 4.0
time_step = 0.08
coupling = 0.5

MESH = pl.DeviceIdType.MESH
F32 = jnp.float32
BF16 = jnp.bfloat16
X = 8
CELLS = 1024
LT = CELLS // 128
NVD = 32
LV = 128
CH = 56
FIELD_ROWS = (1, 2, 3, 4, 0, 10, 11, 12)
OTHER_ROWS = (0, 5, 6, 7, 8, 9, 10, 11, 12)
HIGHEST = lax.Precision.HIGHEST


def functions_of(cx, cy, cz, xp):
    square = cx * cx + cy * cy + cz * cz
    weights = (2.0 * speed_range / NVX) ** 3 * math.pi ** (-1.5) * xp.exp(-square)
    heat = square - 2.5
    one = xp.ones_like(cx)
    rows = xp.stack(
        [
            one, cx, cy, cz, 2.0 * square / 3.0 - 1.0,
            2.0 * cx * cy, 2.0 * cx * cz, 2.0 * cy * cz,
            cx * cx - cy * cy, cy * cy - cz * cz,
            cx * heat, cy * heat, cz * heat,
        ],
        0,
    )
    factor = 4.0 / 15.0
    target = xp.stack(
        [2.0 * cx, 2.0 * cy, 2.0 * cz, square - 1.5, one, factor * cx * heat, factor * cy * heat, factor * cz * heat], 0
    )
    zero = xp.zeros_like(cx)
    centre = 1.0 - time_step * (xp.abs(cx) + xp.abs(cy) + xp.abs(cz))
    stencil = xp.stack(
        [
            centre,
            time_step * xp.maximum(cx, zero), time_step * xp.maximum(-cx, zero),
            time_step * xp.maximum(cy, zero), time_step * xp.maximum(-cy, zero),
            time_step * xp.maximum(cz, zero), time_step * xp.maximum(-cz, zero),
        ],
        0,
    )
    return rows * weights[None], target, stencil


def coupling_table():
    line = speed_range * (2.0 * np.arange(NVX) + 1.0 - NVX) / NVX
    cx, cy, cz = (a.reshape(-1) for a in np.meshgrid(line, line, line, indexing="ij"))
    rows, target, stencil = functions_of(cx, cy, cz, np)
    n = np.einsum("rv,ov,kv->ork", rows, stencil, target)
    planes = list(range(X)) + [-3, -2, -1, X, X + 1, X + 2]
    out = np.zeros((184, 5, 8, 24))
    for i, p in enumerate(planes):
        at = slice(13 * i, 13 * i + 13)
        out[at, 0, :, p + 8] += n[0]
        out[at, 0, :, p + 7] += n[1]
        out[at, 0, :, p + 9] += n[2]
        for j in range(4):
            out[at, 1 + j, :, p + 8] += n[3 + j]
    return np.ascontiguousarray(out.reshape(184, 5, 192).transpose(1, 0, 2)).astype(np.float32)


def split(a):
    hi = a.astype(BF16)
    return hi, (a - hi.astype(F32)).astype(BF16)


def split_table(a):
    hi = lax.reduce_precision(a, exponent_bits=8, mantissa_bits=7)
    return hi.astype(BF16), (a - hi).astype(BF16)


def yz_shifts(x):
    n = x.shape[0]
    lane = lax.broadcasted_iota(jnp.int32, (n, 128), 1)
    t = [x[:, 128 * i:128 * (i + 1)] for i in range(LT)]
    up = [pltpu.roll(a, 16, 1) for a in t]
    down = [pltpu.roll(a, 112, 1) for a in t]
    ylo = [jnp.where(lane < 16, up[i - 1], up[i]) for i in range(LT)]
    yhi = [jnp.where(lane >= 112, down[(i + 1) % LT], down[i]) for i in range(LT)]
    z = lane % NZ
    zlo = [jnp.where(z == 0, pltpu.roll(a, 113, 1), pltpu.roll(a, 1, 1)) for a in t]
    zhi = [jnp.where(z == NZ - 1, pltpu.roll(a, 15, 1), pltpu.roll(a, 127, 1)) for a in t]
    return t, ylo, yhi, zlo, zhi


def cat(parts):
    return jnp.concatenate(parts, axis=1)


def stencil_moments(q_ref, p):
    def rows(o):
        return q_ref[p, 16 * o:16 * o + 16, :]

    total = rows(0)
    ylo = yz_one(rows(3), 0)
    yhi = yz_one(rows(4), 1)
    zlo = yz_one(rows(5), 2)
    zhi = yz_one(rows(6), 3)
    return total + ylo + yhi + zlo + zhi


def yz_one(x, which):
    n = x.shape[0]
    lane = lax.broadcasted_iota(jnp.int32, (n, 128), 1)
    z = lane % NZ
    t = [x[:, 128 * i:128 * (i + 1)] for i in range(LT)]
    if which == 0:
        up = [pltpu.roll(a, 16, 1) for a in t]
        return cat([jnp.where(lane < 16, up[i - 1], up[i]) for i in range(LT)])
    if which == 1:
        down = [pltpu.roll(a, 112, 1) for a in t]
        return cat([jnp.where(lane >= 112, down[(i + 1) % LT], down[i]) for i in range(LT)])
    if which == 2:
        return cat([jnp.where(z == 0, pltpu.roll(a, 113, 1), pltpu.roll(a, 1, 1)) for a in t])
    return cat([jnp.where(z == NZ - 1, pltpu.roll(a, 15, 1), pltpu.roll(a, 127, 1)) for a in t])


def alpha_of(relax, wall):
    return jnp.where(wall > 0, 0.0, 1.0 - relax)


def stream_rows(src, p, g, ct):
    at = pl.ds(pl.multiple_of(8 * g, 8), 8)
    here, ylo, yhi, zlo, zhi = yz_shifts(src[p, at, :])
    before = src[p - 1, at, :]
    after = src[p + 1, at, :]
    k = [ct[o, at, :] for o in range(7)]
    out = []
    for i in range(LT):
        s = slice(128 * i, 128 * (i + 1))
        a = k[0] * here[i] + k[1] * before[:, s] + k[2] * after[:, s]
        b = k[3] * ylo[i] + k[4] * yhi[i] + k[5] * zlo[i] + k[6] * zhi[i]
        out.append(a + b)
    return out


def exchange(dist_hbm, rw, lm, ct, kx, kb, nc,
             a_out, g1_out, g2_out, mac_out, norm_out,
             dbuf, dt, at_, aa, hl, q1, q2, mine, edges, from_left, from_right, rwl, rwr,
             pbuf, rsbuf, ssum, fbuf, l1, h_out, h_left, h_right, u, b, g1, l2, nsend, nrecv, aleft, aright,
             sem_ld, s_nb, r_nb, s_rs, r_rs, s_ag, r_ag, s_nm, r_nm, sem_out):
    v = lax.axis_index("vel")
    s = lax.axis_index("space")
    left = (v, lax.rem(s + 3, 4))
    right = (v, lax.rem(s + 1, 4))

    loads = [pltpu.make_async_copy(dist_hbm.at[:, pl.ds(128 * t, 128)], dbuf.at[t], sem_ld.at[t]) for t in range(LT)]
    for c in loads:
        c.start()

    barrier = pltpu.get_barrier_semaphore()

    def greet(j, c):
        pl.semaphore_signal(barrier, inc=1, device_id=(lax.rem(v + j, NVD), s), device_id_type=MESH)
        return c

    lax.fori_loop(1, NVD, greet, 0)
    for j in (1, 2, 3):
        pl.semaphore_signal(barrier, inc=1, device_id=(v, lax.rem(s + j, 4)), device_id_type=MESH)

    zero_plane = jnp.zeros((LV, CELLS), F32)
    for p in (0, 1, 10, 11):
        dt[p] = zero_plane
    for p in (0, 1, 12, 13):
        at_[p] = zero_plane

    pl.semaphore_wait(barrier, NVD - 1 + 3)

    def swap(i, to_right, right_dst, to_left, left_dst):
        a = pltpu.make_async_remote_copy(to_right, right_dst, s_nb.at[2 * i], r_nb.at[2 * i],
                                         device_id=right, device_id_type=MESH)
        c = pltpu.make_async_remote_copy(to_left, left_dst, s_nb.at[2 * i + 1], r_nb.at[2 * i + 1],
                                         device_id=left, device_id_type=MESH)
        a.start()
        c.start()
        return a, c

    halo = swap(0, rw, rwl, rw, rwr)
    for c in loads:
        c.wait()

    def first(x, c):
        val = cat([dbuf[t, pl.ds(x, LV, stride=X), :] for t in range(LT)])
        dt[x + 2] = val
        hi, lo = split(val)
        hl[0:LV, :] = hi
        hl[LV:2 * LV, :] = lo
        q = jnp.dot(lm[...], hl[...], preferred_element_type=F32)
        q1[x] = q[0:112] + q[112:224]
        return c

    lax.fori_loop(0, X, first, 0)

    edges[0, 0:16, :] = q1[0, 32:48, :]
    edges[1, 0:16, :] = q1[X - 1, 16:32, :]

    def sum_first(x, c):
        mine[0, x] = stencil_moments(q1, x)
        return c

    lax.fori_loop(0, X, sum_first, 0)
    for x in range(X):
        if x > 0:
            mine[0, x] += q1[x - 1, 16:32, :]
        if x < X - 1:
            mine[0, x] += q1[x + 1, 32:48, :]

    for c in halo:
        c.wait()

    def second(i, c):
        x = i - 1

        def alpha_row(ref, row):
            return alpha_of(ref[pl.ds(row, 1), :], ref[pl.ds(row + X, 1), :])

        inside = jnp.clip(x, 0, X - 1)
        al = alpha_row(rw, inside)
        al = jnp.where(x < 0, alpha_row(rwl, X - 1), al)
        al = jnp.where(x >= X, alpha_row(rwr, 0), al)
        alb = jnp.broadcast_to(al, (8, CELLS))

        def group(g, cc):
            r = stream_rows(dt, i + 1, g, ct)
            at = pl.ds(pl.multiple_of(8 * g, 8), 8)
            at_[i + 2, at, :] = cat(r) * alb
            return cc

        lax.fori_loop(0, LV // 8, group, 0)
        hi, lo = split(at_[i + 2])
        hl[0:LV, :] = hi
        hl[LV:2 * LV, :] = lo
        q = jnp.dot(lm[...], hl[...], preferred_element_type=F32)
        q2[i] = q[0:112] + q[112:224]
        return c

    lax.fori_loop(0, X + 2, second, 0)

    edges[0, 16:32, :] = stencil_moments(q2, 0) + q2[1, 32:48, :]
    edges[0, 32:48, :] = q2[0, 32:48, :]
    edges[1, 16:32, :] = stencil_moments(q2, X + 1) + q2[X, 16:32, :]
    edges[1, 32:48, :] = q2[X + 1, 16:32, :]
    outer = swap(1, edges.at[1], from_left, edges.at[0], from_right)

    def sum_second(x, c):
        mine[1, x] = stencil_moments(q2, x + 1)
        return c

    lax.fori_loop(0, X, sum_second, 0)
    for x in range(X):
        if x > 0:
            mine[1, x] += q2[x, 16:32, :]
        if x < X - 1:
            mine[1, x] += q2[x + 2, 32:48, :]
    for c in outer:
        c.wait()
    mine[0, 0] += from_left[0:16, :]
    mine[1, 0] += from_left[16:32, :]
    mine[1, 1] += from_left[32:48, :]
    mine[0, X - 1] += from_right[0:16, :]
    mine[1, X - 1] += from_right[16:32, :]
    mine[1, X - 2] += from_right[32:48, :]
    pbuf[200:224, :] = jnp.zeros((24, CELLS), F32)
    for m in range(2):
        for x in range(X):
            pbuf[104 * m + 13 * x:104 * m + 13 * x + 13, :] = mine[m, x, 0:13, :]

    def chunk_of(o):
        return (pl.ds(pl.multiple_of(CH * (o // LT), 8), CH), pl.ds(pl.multiple_of(128 * lax.rem(o, LT), 128), 128))

    def send_part(j, c):
        o = lax.rem(v + j, NVD)
        rows, cols = chunk_of(o)
        pltpu.make_async_remote_copy(pbuf.at[rows, cols], rsbuf.at[j], s_rs, r_rs,
                                     device_id=(o, s), device_id_type=MESH).start()
        return c

    lax.fori_loop(1, NVD, send_part, 0)

    def third(i, c):
        def group(g, cc):
            r = stream_rows(at_, i + 1, g, ct)
            at = pl.ds(pl.multiple_of(8 * g, 8), 8)
            aa[i, at, :] = cat(r)
            return cc

        lax.fori_loop(0, LV // 8, group, 0)
        return c

    lax.fori_loop(0, X + 4, third, 0)
    edge_rows = swap(2, aa.at[pl.ds(10, 2)], aleft, aa.at[pl.ds(0, 2)], aright)

    all_parts = rsbuf.at[pl.ds(1, NVD - 1)]
    pltpu.make_async_copy(all_parts, all_parts, r_rs).wait()
    rows, cols = chunk_of(v)
    total = pbuf[rows, cols]

    def add_part(j, acc):
        return acc + rsbuf[j]

    total = lax.fori_loop(1, NVD, add_part, total)
    ssum[...] = total
    fbuf[rows, cols] = total
    def send_sum(j, c):
        o = lax.rem(v + j, NVD)
        pltpu.make_async_remote_copy(ssum, fbuf.at[rows, cols], s_ag, r_ag,
                                     device_id=(o, s), device_id_type=MESH).start()
        return c

    lax.fori_loop(1, NVD, send_sum, 0)
    pltpu.make_async_copy(all_parts, all_parts, s_rs).wait()
    pltpu.make_async_copy(all_parts, all_parts, r_ag).wait()

    f1 = fbuf[0:104, :]
    l1[...] = jnp.dot(kx[...], f1, precision=HIGHEST, preferred_element_type=F32)
    l20 = jnp.dot(kx[0:32, :], fbuf[104:208, :], precision=HIGHEST, preferred_element_type=F32)
    h_out[0:64, :] = l1[0:64, :]
    h_out[64:96, :] = l20
    halo2 = swap(3, h_out, h_left, h_out, h_right)
    for c in halo2:
        c.wait()

    zero8 = jnp.zeros((8, CELLS), F32)

    def clear_ends(k, c):
        for i in range(2):
            u[i, k, 0:8, :] = zero8
            u[i, k, 32:40, :] = zero8
        return c

    lax.fori_loop(0, 4, clear_ends, 0)

    def smooth():
        def start(k, c):
            u[0, k, 8:32, :] = b[k]
            return c

        lax.fori_loop(0, 4, start, 0)
        for sweep in range(SWEEPS):
            src, dst = sweep % 2, 1 - sweep % 2

            def row(k, c):
                for blk in range(3):
                    lo = 8 + 8 * blk
                    here, ylo, yhi, zlo, zhi = yz_shifts(u[src, k, lo:lo + 8, :])
                    before = u[src, k, lo - 1:lo + 7, :]
                    after = u[src, k, lo + 1:lo + 9, :]
                    side = cat([ylo[i] + yhi[i] + zlo[i] + zhi[i] for i in range(LT)])
                    near = before + after + side
                    u[dst, k, lo:lo + 8, :] = (b[k, 8 * blk:8 * blk + 8, :] + coupling * near) * (1.0 / (1.0 + 6.0 * coupling))
                return c

            lax.fori_loop(0, 4, row, 0)
        return SWEEPS % 2

    for k in range(4):
        b[k, 0:8, :] = h_left[8 * k:8 * k + 8, :]
        b[k, 8:16, :] = l1[8 * k:8 * k + 8, :]
        b[k, 16:24, :] = h_right[8 * k:8 * k + 8, :]
    last = smooth()

    plane = lax.broadcasted_iota(jnp.int32, (8, CELLS), 0)

    def gammas(ref):
        relax, wall = ref[0:X, :], ref[X:2 * X, :]
        beta = jnp.where(wall > 0, 0.0, relax)
        return beta, jnp.where(wall > 0, 1.0, relax)

    for blk, ref in enumerate((rwl, rw, rwr)):
        beta, both = gammas(ref)
        keep = plane >= 4 if blk == 0 else (plane < 4 if blk == 2 else None)
        for k in range(8):
            if k < 4:
                f = u[last, k, 8 + 8 * blk:16 + 8 * blk, :]
            elif blk == 0:
                f = h_left[8 * k:8 * k + 8, :]
            elif blk == 1:
                f = l1[8 * k:8 * k + 8, :]
            else:
                f = h_right[8 * k:8 * k + 8, :]
            val = f * (both if k in (3, 4) else beta)
            if keep is not None:
                val = jnp.where(keep, val, 0.0)
            g1[24 * k + 8 * blk:24 * k + 8 * blk + 8, :] = val
    send_g1 = pltpu.make_async_copy(g1, g1_out, sem_out.at[0])
    send_g1.start()

    def squares(l, sm):
        total = jnp.zeros((8, CELLS), F32)
        for i in range(9):
            d = l[64 + 8 * i:72 + 8 * i, :]
            total = total + d * d
        for k in range(4):
            d = u[sm, k, 16:24, :] - l[136 + 8 * k:144 + 8 * k, :]
            total = total + d * d
        out = total[:, 0:128]
        for i in range(1, LT):
            out = out + total[:, 128 * i:128 * (i + 1)]
        return out

    n1 = squares(l1, last)

    add = jnp.dot(nc[0], g1[...], precision=HIGHEST, preferred_element_type=F32)
    for j in range(4):
        add = add + jnp.dot(nc[1 + j], yz_one(g1[...], j), precision=HIGHEST, preferred_element_type=F32)
    m2 = fbuf[104:208, :] + add[0:104]
    l2[...] = jnp.dot(kx[...], m2, precision=HIGHEST, preferred_element_type=F32)
    edge = jnp.dot(kb[...], add[104:184], precision=HIGHEST, preferred_element_type=F32)
    for k in range(4):
        b[k, 0:8, :] = jnp.where(plane >= 5, h_left[64 + 8 * k:72 + 8 * k, :] + edge[8 * k:8 * k + 8], 0.0)
        b[k, 8:16, :] = l2[8 * k:8 * k + 8, :]
        b[k, 16:24, :] = jnp.where(plane < 3, h_right[64 + 8 * k:72 + 8 * k, :] + edge[32 + 8 * k:40 + 8 * k], 0.0)
    last = smooth()
    n2 = squares(l2, last)
    nsend[0] = n1
    nsend[1] = n2
    notes = []
    for j in (1, 2, 3):
        c = pltpu.make_async_remote_copy(nsend, nrecv.at[j - 1], s_nm.at[j - 1], r_nm.at[j - 1],
                                         device_id=(v, lax.rem(s + j, 4)), device_id_type=MESH)
        c.start()
        notes.append(c)

    beta, both = gammas(rw)
    for k in range(8):
        f = u[last, k, 16:24, :] if k < 4 else l2[8 * k:8 * k + 8, :]
        g2_out[8 * k:8 * k + 8, :] = f * (both if k in (3, 4) else beta)

    tile = pl.ds(pl.multiple_of(128 * (v // 4), 128), 128)
    turn = lax.rem(128 - 32 * lax.rem(v, 4), 128)
    for r in range(MOM):
        if 1 <= r <= 4:
            f = u[last, r - 1, 16:24, tile]
        elif r == 0:
            f = l2[32:40, tile]
        elif r >= 10:
            f = l2[40 + 8 * (r - 10):48 + 8 * (r - 10), tile]
        else:
            f = l2[168 + 8 * (r - 5):176 + 8 * (r - 5), tile]
        mac_out[r] = pltpu.roll(f, turn, 1)[:, 0:32]

    for c in edge_rows:
        c.wait()
    for i in range(2):
        aa[2 + i] += aleft[i]
        aa[8 + i] += aright[i]
    send_a = pltpu.make_async_copy(aa.at[pl.ds(2, X)], a_out, sem_out.at[1])
    send_a.start()

    for c in notes:
        c.wait()
    both_n = [nsend[i] + nrecv[0, i] + nrecv[1, i] + nrecv[2, i] for i in range(2)]
    sums = [jnp.sqrt(jnp.sum(t)) for t in both_n]
    lane = lax.broadcasted_iota(jnp.int32, (8, 128), 1)
    norm_out[...] = jnp.where(lane == 0, sums[0], sums[1])
    send_g1.wait()
    send_a.wait()
    pltpu.make_async_copy(all_parts, all_parts, s_ag).wait()


PAIRS = 4


def renew(a_hbm, g1_ref, g2_ref, rw_ref, lt_ref, out_hbm, abuf, obuf, stage, rhs, sem_in, sem_out):
    fetch = [
        pltpu.make_async_copy(a_hbm.at[:, :, pl.ds(256 * i, 256)], abuf.at[i], sem_in.at[i]) for i in range(PAIRS)
    ]
    for c in fetch:
        c.start()
    alpha = alpha_of(rw_ref[0:X, :], rw_ref[X:2 * X, :])

    for k in range(8):
        here, ylo, yhi, zlo, zhi = yz_shifts(g1_ref[24 * k + 8:24 * k + 16, :])
        before = g1_ref[24 * k + 7:24 * k + 15, :]
        after = g1_ref[24 * k + 9:24 * k + 17, :]
        for t in range(LT):
            cols = slice(128 * t, 128 * (t + 1))
            vals = (here[t], before[:, cols], after[:, cols], ylo[t], yhi[t], zlo[t], zhi[t])
            for o, val in enumerate(vals):
                stage[t, 64 * o + 8 * k:64 * o + 8 * k + 8, :] = val * alpha[:, cols]
            stage[t, 448 + 8 * k:456 + 8 * k, :] = g2_ref[8 * k:8 * k + 8, cols]

    def spread(x, c):
        for t in range(LT):
            hi, lo = split(stage[t, pl.ds(x, 64, stride=X), :])
            cols = slice(128 * t, 128 * (t + 1))
            rhs[x, 0:64, cols] = hi
            rhs[x, 64:128, cols] = lo
            rhs[x, 128:192, cols] = hi
            rhs[x, 192:256, cols] = lo
        return c

    lax.fori_loop(0, X, spread, 0)

    puts = []
    for i in range(PAIRS):
        fetch[i].wait()

        def plane(x, c):
            al = alpha_of(rw_ref[pl.ds(x, 1), 256 * i:256 * (i + 1)], rw_ref[pl.ds(x + X, 1), 256 * i:256 * (i + 1)])
            val = jnp.dot(lt_ref[...], rhs[x, :, 256 * i:256 * (i + 1)], preferred_element_type=F32) + al * abuf[i, x]
            obuf[2 * i, pl.ds(x, LV, stride=X), :] = val[:, 0:128]
            obuf[2 * i + 1, pl.ds(x, LV, stride=X), :] = val[:, 128:256]
            return c

        lax.fori_loop(0, X, plane, 0)
        for t in (2 * i, 2 * i + 1):
            c = pltpu.make_async_copy(obuf.at[t], out_hbm.at[:, pl.ds(128 * t, 128)], sem_out.at[t])
            c.start()
            puts.append(c)
    for c in puts:
        c.wait()


def shards(nc, dist, vel_index, relax, wall_mask, macro_inverse):
    velocity = speed_range * (2.0 * vel_index.astype(F32) + 1.0 - NVX) / NVX
    rows, target, stencil = functions_of(velocity[0], velocity[1], velocity[2], jnp)
    rows16 = jnp.concatenate([rows, jnp.zeros((3, LV), F32)], 0)
    lm = (stencil[:, None, :] * rows16[None]).reshape(112, LV)
    hi, lo = split_table(lm)
    lm = jnp.concatenate([jnp.concatenate([hi, hi], 1), jnp.concatenate([lo, jnp.zeros_like(lo)], 1)], 0)
    ct = jnp.broadcast_to(stencil[:, :, None], (7, LV, 128))
    lt = jnp.concatenate([(stencil[:, None, :] * target[None]).reshape(56, LV), target], 0).T
    hi, lo = split_table(lt)
    lt = jnp.concatenate([hi, hi, lo, lo], 1)

    eye = jnp.eye(X, dtype=F32)
    ident = jnp.eye(MOM, dtype=F32)
    table = jnp.concatenate(
        [macro_inverse[jnp.array(FIELD_ROWS)], (macro_inverse - ident)[jnp.array(OTHER_ROWS)], ident[1:5], macro_inverse[5:10]], 0
    )
    kx = (table[:, None, None, :] * eye[None, :, :, None]).reshape(26 * X, X * MOM)
    place = np.zeros((2, 8, 6), np.float32)
    for i in range(3):
        place[0, 5 + i, i] = 1.0
        place[1, i, 3 + i] = 1.0
    kb = (macro_inverse[1:5][None, :, None, None, :] * place[:, None, :, :, None]).reshape(64, 78)
    kb = jnp.concatenate([kb, jnp.zeros((64, 2), F32)], 1)
    rw = jnp.concatenate([relax, wall_mask.astype(F32)], 0)

    vmem = pl.BlockSpec(memory_space=pltpu.VMEM)
    hbm = pl.BlockSpec(memory_space=pl.ANY)
    dma = pltpu.SemaphoreType.DMA
    sds = jax.ShapeDtypeStruct
    a, g1, g2, mac, norm = pl.pallas_call(
        exchange,
        out_shape=(
            sds((X, LV, CELLS), F32), sds((192, CELLS), F32), sds((64, CELLS), F32),
            sds((MOM, X, 32), F32), sds((8, 128), F32),
        ),
        in_specs=[hbm] + [vmem] * 6,
        out_specs=(hbm, hbm, vmem, vmem, vmem),
        scratch_shapes=[
            pltpu.VMEM((LT, LV * X, 128), F32),
            pltpu.VMEM((X + 4, LV, CELLS), F32),
            pltpu.VMEM((X + 6, LV, CELLS), F32),
            pltpu.VMEM((X + 4, LV, CELLS), F32),
            pltpu.VMEM((2 * LV, CELLS), BF16),
            pltpu.VMEM((X, 112, CELLS), F32),
            pltpu.VMEM((X + 2, 112, CELLS), F32),
            pltpu.VMEM((2, X, 16, CELLS), F32),
            pltpu.VMEM((2, 48, CELLS), F32),
            pltpu.VMEM((48, CELLS), F32),
            pltpu.VMEM((48, CELLS), F32),
            pltpu.VMEM((2 * X, CELLS), F32),
            pltpu.VMEM((2 * X, CELLS), F32),
            pltpu.VMEM((4 * CH, CELLS), F32),
            pltpu.VMEM((NVD, CH, 128), F32),
            pltpu.VMEM((CH, 128), F32),
            pltpu.VMEM((4 * CH, CELLS), F32),
            pltpu.VMEM((26 * X, CELLS), F32),
            pltpu.VMEM((96, CELLS), F32),
            pltpu.VMEM((96, CELLS), F32),
            pltpu.VMEM((96, CELLS), F32),
            pltpu.VMEM((2, 4, 40, CELLS), F32),
            pltpu.VMEM((4, 24, CELLS), F32),
            pltpu.VMEM((192, CELLS), F32),
            pltpu.VMEM((26 * X, CELLS), F32),
            pltpu.VMEM((2, 8, 128), F32),
            pltpu.VMEM((3, 2, 8, 128), F32),
            pltpu.VMEM((2, LV, CELLS), F32),
            pltpu.VMEM((2, LV, CELLS), F32),
            dma((LT,)), dma((8,)), dma((8,)), dma, dma, dma, dma, dma((3,)), dma((3,)), dma((2,)),
        ],
        compiler_params=pltpu.CompilerParams(collective_id=0, has_side_effects=True, vmem_limit_bytes=60 * 2 ** 20),
        name="exchange",
    )(dist.reshape(LV * X, CELLS), rw, lm, ct, kx, kb, nc)

    out = pl.pallas_call(
        renew,
        out_shape=sds((LV * X, CELLS), F32),
        in_specs=[hbm] + [vmem] * 4,
        out_specs=hbm,
        scratch_shapes=[
            pltpu.VMEM((PAIRS, X, LV, 256), F32),
            pltpu.VMEM((LT, LV * X, 128), F32),
            pltpu.VMEM((LT, 512, 128), F32),
            pltpu.VMEM((X, 256, CELLS), BF16),
            dma((PAIRS,)), dma((LT,)),
        ],
        compiler_params=pltpu.CompilerParams(vmem_limit_bytes=40 * 2 ** 20),
        name="renew",
    )(a, g1, g2, rw, lt)
    return (out.reshape(LV, X, CELLS), mac, norm[0, 0:2])


def solution(mesh):
    nc = coupling_table()
    return jax.shard_map(
        lambda *args: shards(jnp.asarray(nc), *args),
        mesh=mesh,
        in_specs=(P("vel", "space", None), P(None, "vel"), P("space", None), P("space", None), P()),
        out_specs=(P("vel", "space", None), P(None, "space", "vel"), P()),
        check_vma=False,
    )
```

time: 977 us -> 160 us (0.16)
  the two profiles are of different devices: /device:TPU:1 before, /device:TPU:121 now
where the time goes in v1:
time: 160 us; the launch traced here: 159 us
  Pallas kernels  137 us (86%)
  local copies, waits for them, and re-layouts  14.2 us (9%)
  other arithmetic  6.86 us (4%)
    pallas_call x1, Pallas kernels, shards(): pl.pallas_call(exchange, out_shape=(sds((X, LV, CELLS), F32), sds((192, C...  128 us
    pallas_call x1, Pallas kernels, shards(): pl.pallas_call(renew, out_shape=sds((LV * X, CELLS), F32), in_specs=[hbm]...  9.27 us
    unnamed x14, local copies, waits for them, and re-layouts  5.23 us

profile of v1, /device:TPU:121, one launch (start us, length us, event | category | flops | bytes accessed | tf_op | source)
XLA Modules:
  0.0 159.2 jit_solution(8619832299813566928)
XLA Ops:
  0.6 0.7 add_multiply_fusion
  1.3 0.7 slice.27
  2.0 0.7 pad_clamp_fusion.1
  2.7 1.2 gather_fusion
  3.9 0.7 pad_clamp_fusion
  4.6 0.7 slice.26
  5.3 0.7 fusion.6
  6.0 0.6 gather_fusion.1
  6.6 0.8 convert_element_type.30
  7.4 1.4 pad_maximum_fusion.rw.rw_ref
  8.8 0.1 copy.123
  8.9 0.1 copy.124
  9.0 0.1 copy.125
  9.1 0.8 broadcast_multiply_fusion.1
  9.9 0.1 mul.272
  10.0 0.6 concatenate.34.kb
  10.7 0.1 copy.87
  10.8 0.1 copy.93
  10.9 0.1 copy.92
  11.0 0.1 copy.116
  11.0 0.1 copy.120
  11.1 0.1 copy.94
  11.2 0.2 multiply_multiply_fusion.1
  11.4 0.1 copy.104
  11.5 0.1 copy.96
  11.5 0.1 copy.101
  11.6 0.1 copy.103
  11.7 0.1 copy.89
  11.8 0.1 copy.88
  11.9 0.1 copy.108
  11.9 0.1 copy.91
  12.0 0.1 copy.90
  12.2 0.1 copy.118
  12.3 0.1 copy.117
  12.5 0.1 copy.121
  12.6 0.2 concatenate.35
  12.9 0.1 pad_maximum_fusion.1.lt_ref
  13.0 0.7 fusion.1.lm
  13.7 1.0 broadcast_in_dim.9.ct
  14.6 0.2 broadcast_multiply_fusion
  14.8 0.9 mul.267.kx
  15.7 128.1 %exchange.1 = (f32[8,128,1024]{2,1,0:T(8,128)}, f32[192,1024]{1,0:T(8,128)}, f32[64,1024]{1,0:T(8,128)}, f32[13,8,32]{2,1,0:T(8,128)}, f32[8,128]{1,0:T(8,128)}) custom-call(f32[1024,1024]{1,0:T(8,128)} %bitcast.15, f32[16,1024]{1,0:T(8,128)} %pad_maximum_fusion.rw.rw_ref, bf16[224,256]{1,0:T(8,128)(2,1)} %fusion.1.lm, f32[7,128,128]{2,1,0:T(8,128)} %broadcast_in_dim.9.ct, ...), custom_call_target="tpu_custom_call" | custom-call | tf_op jit(solution)/shard_map/exchange/pallas_call | solution.py:566
  143.9 2.2 %copy-done = f32[8,128,1024]{2,1,0:T(8,128)S(1)} copy-done((f32[8,128,1024]{2,1,0:T(8,128)S(1)}, f32[8,128,1024]{2,1,0:T(8,128)}, u32[]{:S(2)}) %copy-start) | copy-done | bytes 4194328
  146.1 1.1 copy-done.1
  147.2 0.9 copy-done.3
  148.2 9.3 %renew.1 = f32[1024,1024]{1,0:T(8,128)} custom-call(f32[8,128,1024]{2,1,0:T(8,128)S(1)} %copy-done, f32[192,1024]{1,0:T(8,128)S(1)} %copy-done.1, f32[64,1024]{1,0:T(8,128)S(1)} %copy-done.3, f32[16,1024]{1,0:T(8,128)S(1)} %copy-done.2, bf16[128,256]{1,0:T(8,128)(2,1)S(1)} %pad_maximum_fusion.1.lt_ref), custom_call_target="tpu_custom_call" | custom-call | tf_op jit(solution)/shard_map/renew/pallas_call | solution.py:610
  157.4 1.2 slice_bitcast_fusion
  158.6 0.6 copy.129
  (28 shorter events, 0.4 us)
Async XLA Ops:
  13.0 130.9 %copy-start.2 = (f32[16,1024]{1,0:T(8,128)S(1)}, f32[16,1024]{1,0:T(8,128)}, u32[]{:S(2)}) copy-start(f32[16,1024]{1,0:T(8,128)} %pad_maximum_fusion.rw.rw_ref) | copy-start | bytes 196612
  143.9 2.2 %copy-start = (f32[8,128,1024]{2,1,0:T(8,128)S(1)}, f32[8,128,1024]{2,1,0:T(8,128)}, u32[]{:S(2)}) copy-start(f32[8,128,1024]{2,1,0:T(8,128)} %get-tuple-element.8.a_hbm) | copy-start | bytes 12582916
  146.1 1.1 copy-start.1
  147.2 0.9 copy-start.3
  148.1 10.5 %copy-start.4 = (f32[13,8,32]{2,1,0:T(8,128)S(1)}, f32[13,8,32]{2,1,0:T(8,128)}, u32[]{:S(2)}) copy-start(f32[13,8,32]{2,1,0:T(8,128)} %get-tuple-element.60) | copy-start | bytes 39940

commit v2 on v1

v2 whole, which is shorter than its diff:
```python
import functools
import math

import jax
import jax.numpy as jnp
import numpy as np
from jax import lax
from jax.experimental import pallas as pl
from jax.experimental.pallas import tpu as pltpu
from jax.sharding import PartitionSpec as P

NVX = 16
NZ = 16
MOM = 13
SWEEPS = 3
speed_range = 4.0
time_step = 0.08
coupling = 0.5

MESH = pl.DeviceIdType.MESH
F32 = jnp.float32
BF16 = jnp.bfloat16
X = 8
CELLS = 1024
LT = CELLS // 128
RING = 4
PEERS = RING * RING
LV = 128
CH = 56
HALO = 4
EXT = X + 2 * HALO
FIELD_ROWS = (1, 2, 3, 4, 0, 10, 11, 12)
OTHER_ROWS = (0, 5, 6, 7, 8, 9, 10, 11, 12)
HIGHEST = lax.Precision.HIGHEST


def functions_of(cx, cy, cz, xp=jnp):
    square = cx * cx + cy * cy + cz * cz
    weights = (2.0 * speed_range / NVX) ** 3 * math.pi ** (-1.5) * xp.exp(-square)
    heat = square - 2.5
    one = xp.ones_like(cx)
    rows = [
        one, cx, cy, cz, 2.0 * square / 3.0 - 1.0,
        2.0 * cx * cy, 2.0 * cx * cz, 2.0 * cy * cz,
        cx * cx - cy * cy, cy * cy - cz * cz,
        cx * heat, cy * heat, cz * heat,
    ]
    factor = 4.0 / 15.0
    target = [2.0 * cx, 2.0 * cy, 2.0 * cz, square - 1.5, one, factor * cx * heat, factor * cy * heat, factor * cz * heat]
    stencil = [1.0 - time_step * (xp.abs(cx) + xp.abs(cy) + xp.abs(cz))]
    for c in (cx, cy, cz):
        stencil += [time_step * xp.maximum(c, 0.0), time_step * xp.maximum(-c, 0.0)]
    return [r * weights for r in rows], target, stencil


def selection():
    sel = np.zeros((26, MOM))
    own = np.zeros((26, MOM))
    for j in range(26):
        if j < 8:
            sel[j, FIELD_ROWS[j]] = 1
        elif j < 17:
            sel[j, OTHER_ROWS[j - 8]] = 1
            own[j, OTHER_ROWS[j - 8]] = -1
        elif j < 21:
            own[j, j - 16] = 1
        else:
            sel[j, j - 16] = 1
    eye = np.eye(X)
    sel = np.repeat(sel, X, 0)
    spread = np.tile(np.eye(MOM), (1, X))
    mask = np.repeat(np.tile(eye, (26, 1)), MOM, 1)
    fixed = np.einsum("jr,xp->jxpr", own, eye).reshape(26 * X, X * MOM)
    return [a.astype(np.float32) for a in (sel, spread, mask, fixed)]


def coupling_table():
    line = speed_range * (2.0 * np.arange(NVX) + 1.0 - NVX) / NVX
    cx, cy, cz = (a.reshape(-1) for a in np.meshgrid(line, line, line, indexing="ij"))
    rows, target, stencil = functions_of(cx, cy, cz, np)
    n = np.einsum("rv,ov,kv->ork", rows, stencil, target)
    near = np.zeros((X, MOM, 8, EXT))
    side = np.zeros((X, MOM, 4, 8, X))
    for x in range(X):
        near[x, :, :, x + HALO] += n[0]
        near[x, :, :, x + HALO - 1] += n[1]
        near[x, :, :, x + HALO + 1] += n[2]
        for j in range(4):
            side[x, :, j, :, x] += n[3 + j]
    table = np.concatenate([near.reshape(X * MOM, 8 * EXT), side.reshape(X * MOM, 32 * X)], 1)
    return table.astype(np.float32)


def split(a):
    hi = a.astype(BF16)
    return hi, (a - hi.astype(F32)).astype(BF16)


def cat(parts):
    return jnp.concatenate(parts, axis=1)


def tiles(x):
    return [x[:, 128 * i:128 * (i + 1)] for i in range(LT)]


def y_shifts(t):
    lane = lax.broadcasted_iota(jnp.int32, t[0].shape, 1)
    up = [pltpu.roll(a, 16, 1) for a in t]
    down = [pltpu.roll(a, 112, 1) for a in t]
    ylo = [jnp.where(lane < 16, up[i - 1], up[i]) for i in range(LT)]
    yhi = [jnp.where(lane >= 112, down[(i + 1) % LT], down[i]) for i in range(LT)]
    return ylo, yhi


def z_shifts(t):
    z = lax.broadcasted_iota(jnp.int32, t[0].shape, 1) % NZ
    zlo = [jnp.where(z == 0, pltpu.roll(a, 113, 1), pltpu.roll(a, 1, 1)) for a in t]
    zhi = [jnp.where(z == NZ - 1, pltpu.roll(a, 15, 1), pltpu.roll(a, 127, 1)) for a in t]
    return zlo, zhi


def yz_shifts(x):
    t = tiles(x)
    return (t,) + y_shifts(t) + z_shifts(t)


def stencil_moments(q_ref, p):
    def rows(o, at=p):
        return tiles(q_ref[at, 16 * o:16 * o + 16, :])

    ylo, _ = y_shifts(rows(3))
    _, yhi = y_shifts(rows(4))
    zlo, _ = z_shifts(rows(5))
    _, zhi = z_shifts(rows(6))
    here, before, after = rows(0), rows(1, p - 1), rows(2, p + 1)
    return cat([(here[i] + before[i] + after[i]) + (ylo[i] + yhi[i]) + (zlo[i] + zhi[i]) for i in range(LT)])


def alpha_of(relax, wall):
    return jnp.where(wall > 0, 0.0, 1.0 - relax)


def stream_plane(src, halves, p, h, ct, zmat, scale=None):
    lane = lax.broadcasted_iota(jnp.int32, (LV, 128), 1)
    k0, cx, cy, cz = (ct[i] for i in range(4))
    px, py, pz = cx > 0, cy > 0, cz > 0
    kx, ky, kz = jnp.abs(cx), jnp.abs(cy), jnp.abs(cz)
    t = [src[p, :, 128 * i:128 * (i + 1)] for i in range(LT)]
    z = [
        jnp.dot(
            cat([halves[h, 0:LV, 128 * i:128 * (i + 1)], halves[h, LV:2 * LV, 128 * i:128 * (i + 1)]]),
            zmat[...],
            preferred_element_type=F32,
        )
        for i in range(LT)
    ]
    up = [pltpu.roll(a, 16, 1) for a in t]
    down = [pltpu.roll(a, 112, 1) for a in t]
    out = []
    for i in range(LT):
        s = slice(128 * i, 128 * (i + 1))
        in_x = jnp.where(px, src[p - 1, :, s], src[p + 1, :, s])
        in_y = jnp.where(
            py,
            jnp.where(lane < 16, up[i - 1], up[i]),
            jnp.where(lane >= 112, down[(i + 1) % LT], down[i]),
        )
        in_z = jnp.where(pz, z[i][:, 0:128], z[i][:, 128:256])
        val = (k0 * t[i] + kx * in_x) + (ky * in_y + kz * in_z)
        out.append(val if scale is None else val * scale[:, s])
    return out


def exchange(dist_hbm, relax_ref, wall_ref, vel_ref, inv_ref, sel_ref, spread_ref, mask_ref, fixed_ref, nc,
             a_out, g1_out, g2_out, mac_out, norm_out,
             dbuf, dt, at_, aa, dhl, ahl, q1, q2, mine, edges, from_left, from_right, rw, rwl, rwr,
             mrows, lm, ct, zmat, kx, pbuf, rsbuf, ssum, xbuf, total, fbuf, l1, h_left, h_right, b2out, b2l, b2r,
             u, b, g1, rhs, add, l2, nsend, nrecv, aleft, aright,
             sem_ld, s_nb, r_nb, s_rs, r_rs, s_ag, r_ag, s_x, r_x, s_nm, r_nm, sem_out):
    v = lax.axis_index("vel")
    s = lax.axis_index("space")
    left = (v, lax.rem(s + 3, 4))
    right = (v, lax.rem(s + 1, 4))
    far = v // PEERS
    place = lax.rem(v, PEERS)
    partner = ((1 - far) * PEERS + place, s)

    def peer(o):
        return (far * PEERS + o, s)

    loads = [pltpu.make_async_copy(dist_hbm.at[:, pl.ds(128 * t, 128)], dbuf.at[t], sem_ld.at[t]) for t in range(LT)]
    for c in loads:
        c.start()

    barrier = pltpu.get_barrier_semaphore()

    def greet(j, c):
        pl.semaphore_signal(barrier, inc=1, device_id=peer(lax.rem(place + j, PEERS)), device_id_type=MESH)
        return c

    lax.fori_loop(1, PEERS, greet, 0)
    pl.semaphore_signal(barrier, inc=1, device_id=partner, device_id_type=MESH)
    for j in (1, 2, 3):
        pl.semaphore_signal(barrier, inc=1, device_id=(v, lax.rem(s + j, 4)), device_id_type=MESH)

    rw[0:X, :] = relax_ref[...]
    rw[X:2 * X, :] = wall_ref[...].astype(F32)
    vel = speed_range * (2.0 * vel_ref[...].astype(F32) + 1.0 - NVX) / NVX
    cx, cy, cz = vel[0:1], vel[1:2], vel[2:3]
    rows, _, stencil = functions_of(cx, cy, cz)
    mrows[...] = jnp.zeros_like(mrows)
    for r in range(MOM):
        mrows[r:r + 1, :] = rows[r]
    for o in range(7):
        hi, lo = split(mrows[...] * stencil[o])
        lm[16 * o:16 * o + 16, 0:LV] = hi
        lm[16 * o:16 * o + 16, LV:2 * LV] = hi
        lm[112 + 16 * o:128 + 16 * o, 0:LV] = lo
        lm[112 + 16 * o:128 + 16 * o, LV:2 * LV] = jnp.zeros_like(lo)
    for i, row in enumerate((stencil[0], time_step * cx, time_step * cy, time_step * cz)):
        ct[i] = jnp.transpose(jnp.broadcast_to(row, (LV, LV)))
    src_lane = lax.broadcasted_iota(jnp.int32, (LV, LV), 0)
    dst_lane = lax.broadcasted_iota(jnp.int32, (LV, LV), 1)
    dst_z = dst_lane % NZ
    lower = jnp.where(src_lane == jnp.where(dst_z == 0, dst_lane + NZ - 1, dst_lane - 1), 1.0, 0.0).astype(BF16)
    upper = jnp.where(src_lane == jnp.where(dst_z == NZ - 1, dst_lane - NZ + 1, dst_lane + 1), 1.0, 0.0).astype(BF16)
    for i in range(2):
        zmat[LV * i:LV * (i + 1), 0:LV] = lower
        zmat[LV * i:LV * (i + 1), LV:2 * LV] = upper
    part = jnp.dot(sel_ref[...], inv_ref[...], precision=HIGHEST, preferred_element_type=F32)
    part = jnp.dot(part, spread_ref[...], precision=HIGHEST, preferred_element_type=F32)
    kx[...] = part * mask_ref[...] + fixed_ref[...]
    zero_plane = jnp.zeros((LV, CELLS), F32)
    for p in (0, 9):
        dt[p] = zero_plane
        q1[p, 16:48, :] = jnp.zeros((32, CELLS), F32)
    for p in (0, 11):
        at_[p] = zero_plane
    for m in range(2):
        pbuf[m, 104:112, :] = jnp.zeros((8, CELLS), F32)

    pl.semaphore_wait(barrier, PEERS - 1 + 1 + 3)

    def swap(i, to_right, right_dst, to_left, left_dst):
        a = pltpu.make_async_remote_copy(to_right, right_dst, s_nb.at[2 * i], r_nb.at[2 * i],
                                         device_id=right, device_id_type=MESH)
        c = pltpu.make_async_remote_copy(to_left, left_dst, s_nb.at[2 * i + 1], r_nb.at[2 * i + 1],
                                         device_id=left, device_id_type=MESH)
        a.start()
        c.start()
        return a, c

    def settle(copies):
        for c in copies:
            c.wait()

    halo = swap(0, rw, rwl, rw, rwr)
    settle(loads)

    def first(x, c):
        val = cat([dbuf[t, pl.ds(x, LV, stride=X), :] for t in range(LT)])
        dt[x + 1] = val
        hi, lo = split(val)
        dhl[x, 0:LV, :] = hi
        dhl[x, LV:2 * LV, :] = lo
        q = jnp.dot(lm[...], dhl[x], preferred_element_type=F32)
        q1[x + 1] = q[0:112] + q[112:224]
        return c

    lax.fori_loop(0, X, first, 0)
    edges[0, 0:16, :] = q1[1, 32:48, :]
    edges[1, 0:16, :] = q1[X, 16:32, :]
    outer1 = swap(1, edges.at[1, pl.ds(0, 16)], from_left.at[pl.ds(0, 16)],
                  edges.at[0, pl.ds(0, 16)], from_right.at[pl.ds(0, 16)])

    def sum_first(x, c):
        mine[0, x] = stencil_moments(q1, x + 1)
        return c

    lax.fori_loop(0, X, sum_first, 0)
    settle(halo)

    def alpha_row(ref, x):
        return alpha_of(ref[pl.ds(x, 1), :], ref[pl.ds(x + X, 1), :])

    def products(i):
        hi, lo = split(at_[i + 1])
        ahl[i, 0:LV, :] = hi
        ahl[i, LV:2 * LV, :] = lo
        q = jnp.dot(lm[...], ahl[i], preferred_element_type=F32)
        q2[i] = q[0:112] + q[112:224]

    def second(j, c):
        x = lax.rem(X - j, X)
        val = stream_plane(dt, dhl, x + 1, x, ct, zmat, alpha_row(rw, x))
        for i in range(LT):
            at_[x + 2, :, 128 * i:128 * (i + 1)] = val[i]
        products(x + 1)
        return c

    lax.fori_loop(0, 2, second, 0)
    speed = ct[1]
    to_lower = jnp.where(speed > 0, 0.0, -speed)
    to_upper = jnp.where(speed > 0, speed, 0.0)
    al_l, al_r = alpha_row(rwl, X - 1), alpha_row(rwr, 0)
    for i in range(LT):
        c = slice(128 * i, 128 * (i + 1))
        at_[1, :, c] = to_lower * dt[1, :, c] * al_l[:, c]
        at_[X + 2, :, c] = to_upper * dt[X, :, c] * al_r[:, c]

    def ends(j, c):
        products((X + 1) * j)
        return c

    lax.fori_loop(0, 2, ends, 0)

    def third(i):
        val = stream_plane(at_, ahl, i + 1, i, ct, zmat)
        for t in range(LT):
            aa[i + 1, :, 128 * t:128 * (t + 1)] = val[t]

    def edge_third(j, c):
        third((X + 1) * j)
        return c

    lax.fori_loop(0, 2, edge_third, 0)
    for i in range(LT):
        c = slice(128 * i, 128 * (i + 1))
        aa[0, :, c] = to_lower * at_[1, :, c]
        aa[X + 3, :, c] = to_upper * at_[X + 2, :, c]

    settle(outer1)
    mine[0, 0] += from_left[0:16, :]
    mine[0, X - 1] += from_right[0:16, :]

    def pack(m):
        for x in range(X):
            pbuf[m, 13 * x:13 * x + 13, :] = mine[m, x, 0:13, :]

    def chunk_of(o):
        return (pl.ds(pl.multiple_of(CH * (o // LT), 8), CH), pl.ds(pl.multiple_of(128 * lax.rem(o, LT), 128), 128))

    def send_parts(m):
        def send(j, c):
            o = lax.rem(place + j, PEERS)
            r, k = chunk_of(o)
            pltpu.make_async_remote_copy(pbuf.at[m, r, k], rsbuf.at[m, j], s_rs.at[m], r_rs.at[m],
                                         device_id=peer(o), device_id_type=MESH).start()
            return c

        lax.fori_loop(1, PEERS, send, 0)

    def all_parts(m):
        return rsbuf.at[m, pl.ds(1, PEERS - 1)]

    def across(m):
        return pltpu.make_async_remote_copy(ssum.at[m], xbuf.at[m], s_x.at[m], r_x.at[m],
                                            device_id=partner, device_id_type=MESH)

    def own_sum(m):
        pltpu.make_async_copy(all_parts(m), all_parts(m), r_rs.at[m]).wait()
        r, k = chunk_of(place)
        acc = pbuf[m, r, k]
        for j in range(1, PEERS):
            acc = acc + rsbuf[m, j]
        ssum[m] = acc
        across(m).start()

    def send_total(m):
        across(m).wait()
        val = ssum[m] + xbuf[m]
        total[m] = val
        r, k = chunk_of(place)
        fbuf[m, r, k] = val

        def send(j, c):
            pltpu.make_async_remote_copy(total.at[m], fbuf.at[m, r, k], s_ag.at[m], r_ag.at[m],
                                         device_id=peer(lax.rem(place + j, PEERS)), device_id_type=MESH).start()
            return c

        lax.fori_loop(1, PEERS, send, 0)

    def all_totals(m):
        pltpu.make_async_copy(all_parts(m), all_parts(m), r_ag.at[m]).wait()

    def all_sent(m):
        pltpu.make_async_copy(all_parts(m), all_parts(m), s_rs.at[m]).wait()
        pltpu.make_async_copy(all_parts(m), all_parts(m), s_ag.at[m]).wait()

    pack(0)
    send_parts(0)
    edge_rows = [swap(4, aa.at[X + 2], aleft.at[0], aa.at[0], aright.at[0])]
    lax.fori_loop(2, 7, second, 0)
    own_sum(0)
    lax.fori_loop(7, X, second, 0)

    edges[0, 16:32, :] = stencil_edge(q2, 0) + q2[1, 32:48, :]
    edges[0, 32:48, :] = q2[0, 32:48, :]
    edges[1, 16:32, :] = stencil_edge(q2, X + 1) + q2[X, 16:32, :]
    edges[1, 32:48, :] = q2[X + 1, 16:32, :]
    outer2 = swap(2, edges.at[1, pl.ds(16, 32)], from_left.at[pl.ds(16, 32)],
                  edges.at[0, pl.ds(16, 32)], from_right.at[pl.ds(16, 32)])

    def sum_second(x, c):
        mine[1, x] = stencil_moments(q2, x + 1)
        return c

    lax.fori_loop(0, X, sum_second, 0)
    send_total(0)
    settle(outer2)
    mine[1, 0] += from_left[16:32, :]
    mine[1, 1] += from_left[32:48, :]
    mine[1, X - 1] += from_right[16:32, :]
    mine[1, X - 2] += from_right[32:48, :]
    pack(1)
    send_parts(1)
    edge_rows.append(swap(5, aa.at[X + 3], aleft.at[1], aa.at[1], aright.at[1]))

    def inner_third(i, c):
        third(i)
        return c

    lax.fori_loop(1, X + 1, inner_third, 0)
    own_sum(1)

    all_totals(0)
    l1[...] = jnp.dot(kx[...], fbuf[0, 0:104, :], precision=HIGHEST, preferred_element_type=F32)
    halo2 = swap(3, l1.at[pl.ds(0, 64)], h_left, l1.at[pl.ds(0, 64)], h_right)
    send_total(1)
    settle(halo2)

    zero8 = jnp.zeros((8, CELLS), F32)

    def clear_ends(k, c):
        for i in range(2):
            u[i, k, 0:8, :] = zero8
            u[i, k, 24:32, :] = zero8
        return c

    lax.fori_loop(0, 4, clear_ends, 0)

    def fill(k, lo_rows, own, hi_rows):
        b[k, 0:HALO, :] = lo_rows
        b[k, HALO:HALO + X, :] = own
        b[k, HALO + X:EXT, :] = hi_rows

    def smooth():
        def start(k, c):
            u[0, k, 8:24, :] = b[k]
            return c

        lax.fori_loop(0, 4, start, 0)
        for sweep in range(SWEEPS):
            src, dst = sweep % 2, 1 - sweep % 2

            def row(k, c):
                for blk in range(2):
                    lo = 8 + 8 * blk
                    here, ylo, yhi, zlo, zhi = yz_shifts(u[src, k, lo:lo + 8, :])
                    near = u[src, k, lo - 1:lo + 7, :] + u[src, k, lo + 1:lo + 9, :]
                    side = cat([(ylo[i] + yhi[i]) + (zlo[i] + zhi[i]) for i in range(LT)])
                    u[dst, k, lo:lo + 8, :] = (b[k, 8 * blk:8 * blk + 8, :] + coupling * (near + side)) * (1.0 / (1.0 + 6.0 * coupling))
                return c

            lax.fori_loop(0, 4, row, 0)
        return SWEEPS % 2

    for k in range(4):
        fill(k, h_left[8 * k + 4:8 * k + 8, :], l1[8 * k:8 * k + 8, :], h_right[8 * k:8 * k + 4, :])
    last = smooth()

    def gammas(relax, wall):
        return jnp.where(wall > 0, 0.0, relax), jnp.where(wall > 0, 1.0, relax)

    factors = [gammas(ref[0:X, :], ref[X:2 * X, :]) for ref in (rwl, rw, rwr)]
    for k in range(8):
        gl, go, gr = (f[1 if k in (3, 4) else 0] for f in factors)
        if k < 4:
            lo_rows = u[last, k, 8:8 + HALO, :]
            own = u[last, k, 8 + HALO:8 + HALO + X, :]
            hi_rows = u[last, k, 8 + HALO + X:8 + EXT, :]
        else:
            lo_rows = h_left[8 * k + 4:8 * k + 8, :]
            own = l1[8 * k:8 * k + 8, :]
            hi_rows = h_right[8 * k:8 * k + 4, :]
        own = own * go
        g1[EXT * k:EXT * k + HALO, :] = lo_rows * gl[4:8]
        g1[EXT * k + HALO:EXT * k + HALO + X, :] = own
        g1[EXT * k + HALO + X:EXT * (k + 1), :] = hi_rows * gr[0:4]
        _, ylo, yhi, zlo, zhi = yz_shifts(own)
        for j, val in enumerate((ylo, yhi, zlo, zhi)):
            rhs[64 * j + 8 * k:64 * j + 8 * k + 8, :] = cat(val)
    send_g1 = pltpu.make_async_copy(g1, g1_out, sem_out.at[0])
    send_g1.start()

    def squares(l, sm):
        acc = jnp.zeros((8, CELLS), F32)
        for i in range(9):
            d = l[64 + 8 * i:72 + 8 * i, :]
            acc = acc + d * d
        for k in range(4):
            d = u[sm, k, 8 + HALO:8 + HALO + X, :] - l[136 + 8 * k:144 + 8 * k, :]
            acc = acc + d * d
        parts = tiles(acc)
        out = parts[0]
        for i in range(1, LT):
            out = out + parts[i]
        return out

    nsend[0] = squares(l1, last)

    add[...] = (
        jnp.dot(nc[:, 0:128], g1[...], precision=HIGHEST, preferred_element_type=F32)
        + jnp.dot(nc[:, 128:384], rhs[...], precision=HIGHEST, preferred_element_type=F32)
    )
    all_totals(1)
    m2 = fbuf[1, 0:104, :] + add[...]
    b2out[...] = jnp.dot(kx[0:32, :], m2, precision=HIGHEST, preferred_element_type=F32)
    halo3 = swap(6, b2out, b2l, b2out, b2r)
    l2[...] = jnp.dot(kx[32:208, :], m2, precision=HIGHEST, preferred_element_type=F32)

    for c in edge_rows:
        settle(c)
    for i in range(2):
        aa[2 + i] += aleft[i]
    aa[X] += aright[0]
    aa[X + 1] += aright[1]
    send_a = pltpu.make_async_copy(aa.at[pl.ds(2, X)], a_out, sem_out.at[1])
    send_a.start()

    settle(halo3)
    for k in range(4):
        fill(k, b2l[8 * k + 4:8 * k + 8, :], b2out[8 * k:8 * k + 8, :], b2r[8 * k:8 * k + 4, :])
    last = smooth()
    acc = jnp.zeros((8, CELLS), F32)
    for i in range(9):
        d = l2[32 + 8 * i:40 + 8 * i, :]
        acc = acc + d * d
    for k in range(4):
        d = u[last, k, 8 + HALO:8 + HALO + X, :] - l2[104 + 8 * k:112 + 8 * k, :]
        acc = acc + d * d
    parts = tiles(acc)
    out = parts[0]
    for i in range(1, LT):
        out = out + parts[i]
    nsend[1] = out
    notes = []
    for j in (1, 2, 3):
        c = pltpu.make_async_remote_copy(nsend, nrecv.at[j - 1], s_nm.at[j - 1], r_nm.at[j - 1],
                                         device_id=(v, lax.rem(s + j, 4)), device_id_type=MESH)
        c.start()
        notes.append(c)

    beta, both = gammas(rw[0:X, :], rw[X:2 * X, :])
    for k in range(8):
        f = u[last, k, 8 + HALO:8 + HALO + X, :] if k < 4 else l2[8 * k - 32:8 * k - 24, :]
        g2_out[8 * k:8 * k + 8, :] = f * (both if k in (3, 4) else beta)

    tile = pl.ds(pl.multiple_of(128 * (v // 4), 128), 128)
    turn = lax.rem(128 - 32 * lax.rem(v, 4), 128)
    for r in range(MOM):
        if 1 <= r <= 4:
            f = u[last, r - 1, 8 + HALO:8 + HALO + X, tile]
        elif r == 0:
            f = l2[0:8, tile]
        elif r >= 10:
            f = l2[8 + 8 * (r - 10):16 + 8 * (r - 10), tile]
        else:
            f = l2[136 + 8 * (r - 5):144 + 8 * (r - 5), tile]
        mac_out[r] = pltpu.roll(f, turn, 1)[:, 0:32]

    settle(notes)
    for i in range(2):
        norm_out[i] = (nsend[i] + nrecv[0, i]) + (nrecv[1, i] + nrecv[2, i])
    send_g1.wait()
    send_a.wait()
    for m in range(2):
        all_sent(m)


def stencil_edge(q_ref, p):
    def rows(o):
        return tiles(q_ref[p, 16 * o:16 * o + 16, :])

    ylo, _ = y_shifts(rows(3))
    _, yhi = y_shifts(rows(4))
    zlo, _ = z_shifts(rows(5))
    _, zhi = z_shifts(rows(6))
    here = rows(0)
    return cat([here[i] + (ylo[i] + yhi[i]) + (zlo[i] + zhi[i]) for i in range(LT)])


PAIRS = 4


def renew(a_hbm, g1_ref, g2_ref, relax_ref, wall_ref, vel_ref, mac_ref, sum_ref, out_hbm, mac_out, norm_out,
          abuf, obuf, stage, rhs, lt, lrows, sem_in, sem_out):
    fetch = [
        pltpu.make_async_copy(a_hbm.at[:, :, pl.ds(256 * i, 256)], abuf.at[i], sem_in.at[i]) for i in range(PAIRS)
    ]
    for c in fetch:
        c.start()
    mac_out[...] = mac_ref[...]
    for i in range(2):
        norm_out[i] = jnp.sqrt(jnp.sum(sum_ref[i]))
    alpha = alpha_of(relax_ref[...], wall_ref[...])

    vel = speed_range * (2.0 * vel_ref[...].astype(F32) + 1.0 - NVX) / NVX
    _, target, stencil = functions_of(vel[0:1], vel[1:2], vel[2:3])
    for k in range(8):
        for o in range(7):
            lrows[8 * o + k:8 * o + k + 1, :] = stencil[o] * target[k]
        lrows[56 + k:57 + k, :] = target[k]
    hi, lo = split(lrows[...])
    hi, lo = hi.astype(F32), lo.astype(F32)
    lt[:, 0:128] = jnp.transpose(jnp.concatenate([hi, hi], 0)).astype(BF16)
    lt[:, 128:256] = jnp.transpose(jnp.concatenate([lo, lo], 0)).astype(BF16)

    for k in range(8):
        at = EXT * k + HALO
        here, ylo, yhi, zlo, zhi = yz_shifts(g1_ref[at:at + 8, :])
        before = g1_ref[at - 1:at + 7, :]
        after = g1_ref[at + 1:at + 9, :]
        for t in range(LT):
            cols = slice(128 * t, 128 * (t + 1))
            vals = (here[t], before[:, cols], after[:, cols], ylo[t], yhi[t], zlo[t], zhi[t])
            for o, val in enumerate(vals):
                stage[t, 64 * o + 8 * k:64 * o + 8 * k + 8, :] = val * alpha[:, cols]
            stage[t, 448 + 8 * k:456 + 8 * k, :] = g2_ref[8 * k:8 * k + 8, cols]

    def spread(x, c):
        for t in range(LT):
            hi, lo = split(stage[t, pl.ds(x, 64, stride=X), :])
            cols = slice(128 * t, 128 * (t + 1))
            rhs[x, 0:64, cols] = hi
            rhs[x, 64:128, cols] = lo
            rhs[x, 128:192, cols] = hi
            rhs[x, 192:256, cols] = lo
        return c

    lax.fori_loop(0, X, spread, 0)

    puts = []
    for i in range(PAIRS):
        fetch[i].wait()

        def plane(x, c):
            al = alpha_of(relax_ref[pl.ds(x, 1), 256 * i:256 * (i + 1)], wall_ref[pl.ds(x, 1), 256 * i:256 * (i + 1)])
            val = jnp.dot(lt[...], rhs[x, :, 256 * i:256 * (i + 1)], preferred_element_type=F32) + al * abuf[i, x]
            obuf[2 * i, pl.ds(x, LV, stride=X), :] = val[:, 0:128]
            obuf[2 * i + 1, pl.ds(x, LV, stride=X), :] = val[:, 128:256]
            return c

        lax.fori_loop(0, X, plane, 0)
        for t in (2 * i, 2 * i + 1):
            c = pltpu.make_async_copy(obuf.at[t], out_hbm.at[:, pl.ds(128 * t, 128)], sem_out.at[t])
            c.start()
            puts.append(c)
    for c in puts:
        c.wait()


def shards(consts, dist, vel_index, relax, wall_mask, macro_inverse):
    vmem = pl.BlockSpec(memory_space=pltpu.VMEM)
    hbm = pl.BlockSpec(memory_space=pl.ANY)
    smem = pl.BlockSpec(memory_space=pltpu.SMEM)
    dma = pltpu.SemaphoreType.DMA
    sds = jax.ShapeDtypeStruct
    a, g1, g2, mac, norm = pl.pallas_call(
        exchange,
        out_shape=(
            sds((X, LV, CELLS), F32), sds((8 * EXT, CELLS), F32), sds((64, CELLS), F32),
            sds((MOM, X, 32), F32), sds((2, 8, 128), F32),
        ),
        in_specs=[hbm] + [vmem] * 9,
        out_specs=(hbm, hbm, vmem, vmem, vmem),
        scratch_shapes=[
            pltpu.VMEM((LT, LV * X, 128), F32),
            pltpu.VMEM((X + 2, LV, CELLS), F32),
            pltpu.VMEM((X + 4, LV, CELLS), F32),
            pltpu.VMEM((X + 4, LV, CELLS), F32),
            pltpu.VMEM((X, 2 * LV, CELLS), BF16),
            pltpu.VMEM((X + 2, 2 * LV, CELLS), BF16),
            pltpu.VMEM((X + 2, 112, CELLS), F32),
            pltpu.VMEM((X + 2, 112, CELLS), F32),
            pltpu.VMEM((2, X, 16, CELLS), F32),
            pltpu.VMEM((2, 48, CELLS), F32),
            pltpu.VMEM((48, CELLS), F32),
            pltpu.VMEM((48, CELLS), F32),
            pltpu.VMEM((2 * X, CELLS), F32),
            pltpu.VMEM((2 * X, CELLS), F32),
            pltpu.VMEM((2 * X, CELLS), F32),
            pltpu.VMEM((16, LV), F32),
            pltpu.VMEM((224, 2 * LV), BF16),
            pltpu.VMEM((4, LV, LV), F32),
            pltpu.VMEM((2 * LV, 2 * LV), BF16),
            pltpu.VMEM((26 * X, X * MOM), F32),
            pltpu.VMEM((2, 2 * CH, CELLS), F32),
            pltpu.VMEM((2, PEERS, CH, 128), F32),
            pltpu.VMEM((2, CH, 128), F32),
            pltpu.VMEM((2, CH, 128), F32),
            pltpu.VMEM((2, CH, 128), F32),
            pltpu.VMEM((2, 2 * CH, CELLS), F32),
            pltpu.VMEM((26 * X, CELLS), F32),
            pltpu.VMEM((64, CELLS), F32),
            pltpu.VMEM((64, CELLS), F32),
            pltpu.VMEM((32, CELLS), F32),
            pltpu.VMEM((32, CELLS), F32),
            pltpu.VMEM((32, CELLS), F32),
            pltpu.VMEM((2, 4, 32, CELLS), F32),
            pltpu.VMEM((4, EXT, CELLS), F32),
            pltpu.VMEM((8 * EXT, CELLS), F32),
            pltpu.VMEM((256, CELLS), F32),
            pltpu.VMEM((X * MOM, CELLS), F32),
            pltpu.VMEM((22 * X, CELLS), F32),
            pltpu.VMEM((2, 8, 128), F32),
            pltpu.VMEM((3, 2, 8, 128), F32),
            pltpu.VMEM((2, LV, CELLS), F32),
            pltpu.VMEM((2, LV, CELLS), F32),
            dma((LT,)), dma((14,)), dma((14,)), dma((2,)), dma((2,)), dma((2,)), dma((2,)), dma((2,)), dma((2,)),
            dma((3,)), dma((3,)), dma((2,)),
        ],
        compiler_params=pltpu.CompilerParams(collective_id=0, has_side_effects=True, vmem_limit_bytes=60 * 2 ** 20),
        name="exchange",
    )(dist.reshape(LV * X, CELLS), relax, wall_mask, vel_index, macro_inverse, *consts)

    out, mac, norm = pl.pallas_call(
        renew,
        out_shape=(sds((LV * X, CELLS), F32), sds((MOM, X, 32), F32), sds((2,), F32)),
        in_specs=[hbm] + [vmem] * 7,
        out_specs=(hbm, vmem, smem),
        scratch_shapes=[
            pltpu.VMEM((PAIRS, X, LV, 256), F32),
            pltpu.VMEM((LT, LV * X, 128), F32),
            pltpu.VMEM((LT, 512, 128), F32),
            pltpu.VMEM((X, 256, CELLS), BF16),
            pltpu.VMEM((LV, 256), BF16),
            pltpu.VMEM((64, LV), F32),
            dma((PAIRS,)), dma((LT,)),
        ],
        compiler_params=pltpu.CompilerParams(vmem_limit_bytes=60 * 2 ** 20),
        name="renew",
    )(a, g1, g2, relax, wall_mask, vel_index, mac, norm)
    return (out.reshape(LV, X, CELLS), mac, norm)


def solution(mesh):
    consts = selection() + [coupling_table()]
    return jax.shard_map(
        lambda *args: shards([jnp.asarray(c) for c in consts], *args),
        mesh=mesh,
        in_specs=(P("vel", "space", None), P(None, "vel"), P("space", None), P("space", None), P()),
        out_specs=(P("vel", "space", None), P(None, "space", "vel"), P()),
        check_vma=False,
    )
```

time: 160 us -> 78.8 us (0.49)
  the two profiles are of different devices: /device:TPU:121 before, /device:TPU:1 now
where the time goes in v2:
time: 78.8 us; the launch traced here: 78.6 us
  Pallas kernels  78 us (99%)
    pallas_call x1, Pallas kernels, shards(): pl.pallas_call(exchange, out_shape=(sds((X, LV, CELLS), F32), sds((8 * EX...  67.4 us
    pallas_call x1, Pallas kernels, shards(): pl.pallas_call(renew, out_shape=(sds((LV * X, CELLS), F32), sds((MOM, X,...  10.6 us

profile of v2, /device:TPU:1, one launch (start us, length us, event | category | flops | bytes accessed | tf_op | source)
XLA Modules:
  0.0 78.6 jit_solution(14340432820692941047)
XLA Ops:
  0.6 67.4 %exchange.1 = (f32[8,128,1024]{2,1,0:T(8,128)}, f32[128,1024]{1,0:T(8,128)}, f32[64,1024]{1,0:T(8,128)}, f32[13,8,32]{2,1,0:T(8,128)}, f32[2,8,128]{2,1,0:T(8,128)}) custom-call(f32[1024,1024]{1,0:T(8,128)} %bitcast.2, f32[8,1024]{1,0:T(8,128)} %relax_ref.3, s32[8,1024]{1,0:T(8,128)} %wall_ref.3, s32[3,128]{1,0:T(4,128)} %vel_ref.3, f32[13,13]{1,0:T(8,128)} %inv_ref.1, ...), custom_call_target="tpu_custom_call" | custom-call | tf_op jit(solution)/shard_map/exchange/pallas_call | solution.py:670
  68.0 10.6 %renew.1 = (f32[1024,1024]{1,0:T(8,128)}, f32[13,8,32]{2,1,0:T(8,128)}, f32[2]{0:T(128)}) custom-call(f32[8,128,1024]{2,1,0:T(8,128)} %get-tuple-element.11.a_hbm, f32[128,1024]{1,0:T(8,128)} %get-tuple-element.12.g1_ref, f32[64,1024]{1,0:T(8,128)} %get-tuple-element.13.g2_ref, f32[8,1024]{1,0:T(8,128)} %relax_ref.3, s32[8,1024]{1,0:T(8,128)} %wall_ref.3, ...), custom_call_target="tpu_custom_call" | custom-call | tf_op jit(solution)/shard_map/renew/pallas_call | solution.py:728

commit v3 on v2

--- a/solution.py
+++ b/solution.py
@@ -141,43 +141,43 @@
     return jnp.where(wall > 0, 0.0, 1.0 - relax)
 
 
-def stream_plane(src, halves, p, h, ct, zmat, scale=None):
-    lane = lax.broadcasted_iota(jnp.int32, (LV, 128), 1)
-    k0, cx, cy, cz = (ct[i] for i in range(4))
-    px, py, pz = cx > 0, cy > 0, cz > 0
-    kx, ky, kz = jnp.abs(cx), jnp.abs(cy), jnp.abs(cz)
-    t = [src[p, :, 128 * i:128 * (i + 1)] for i in range(LT)]
-    z = [
-        jnp.dot(
-            cat([halves[h, 0:LV, 128 * i:128 * (i + 1)], halves[h, LV:2 * LV, 128 * i:128 * (i + 1)]]),
-            zmat[...],
-            preferred_element_type=F32,
-        )
-        for i in range(LT)
-    ]
-    up = [pltpu.roll(a, 16, 1) for a in t]
-    down = [pltpu.roll(a, 112, 1) for a in t]
-    out = []
+def stream_plane(src, halves, p, h, ct, zmat, zsel, put, scale=None):
+    pz = ct[3] > 0
     for i in range(LT):
-        s = slice(128 * i, 128 * (i + 1))
-        in_x = jnp.where(px, src[p - 1, :, s], src[p + 1, :, s])
-        in_y = jnp.where(
-            py,
-            jnp.where(lane < 16, up[i - 1], up[i]),
-            jnp.where(lane >= 112, down[(i + 1) % LT], down[i]),
-        )
-        in_z = jnp.where(pz, z[i][:, 0:128], z[i][:, 128:256])
-        val = (k0 * t[i] + kx * in_x) + (ky * in_y + kz * in_z)
-        out.append(val if scale is None else val * scale[:, s])
-    return out
+        c = slice(128 * i, 128 * (i + 1))
+        z = jnp.dot(cat([halves[h, 0:LV, c], halves[h, LV:2 * LV, c]]), zmat[...], preferred_element_type=F32)
+        zsel[:, c] = jnp.where(pz, z[:, 0:128], z[:, 128:256])
+
+    def group(g, carry):
+        at = pl.ds(pl.multiple_of(8 * g, 8), 8)
+        lane = lax.broadcasted_iota(jnp.int32, (8, 128), 1)
+        k0, cx, cy, cz = (ct[i, at, :] for i in range(4))
+        px, py = cx > 0, cy > 0
+        kx, ky, kz = jnp.abs(cx), jnp.abs(cy), jnp.abs(cz)
+        t = [src[p, at, 128 * i:128 * (i + 1)] for i in range(LT)]
+        up = [pltpu.roll(a, 16, 1) for a in t]
+        down = [pltpu.roll(a, 112, 1) for a in t]
+        for i in range(LT):
+            c = slice(128 * i, 128 * (i + 1))
+            in_x = jnp.where(px, src[p - 1, at, c], src[p + 1, at, c])
+            in_y = jnp.where(
+                py,
+                jnp.where(lane < 16, up[i - 1], up[i]),
+                jnp.where(lane >= 112, down[(i + 1) % LT], down[i]),
+            )
+            val = (k0 * t[i] + kx * in_x) + (ky * in_y + kz * zsel[at, c])
+            put(at, c, val if scale is None else val * scale[:, c])
+        return carry
+
+    lax.fori_loop(0, LV // 8, group, 0, unroll=4)
 
 
 def exchange(dist_hbm, relax_ref, wall_ref, vel_ref, inv_ref, sel_ref, spread_ref, mask_ref, fixed_ref, nc,
-             a_out, g1_out, g2_out, mac_out, norm_out,
-             dbuf, dt, at_, aa, dhl, ahl, q1, q2, mine, edges, from_left, from_right, rw, rwl, rwr,
+             aa, g1, g2_out, mac_out, norm_out,
+             dbuf, dt, at_, zsel, dhl, ahl, q1, q2, mine, edges, from_left, from_right, rw, rwl, rwr,
              mrows, lm, ct, zmat, kx, pbuf, rsbuf, ssum, xbuf, total, fbuf, l1, h_left, h_right, b2out, b2l, b2r,
-             u, b, g1, rhs, add, l2, nsend, nrecv, aleft, aright,
-             sem_ld, s_nb, r_nb, s_rs, r_rs, s_ag, r_ag, s_x, r_x, s_nm, r_nm, sem_out):
+             u, b, rhs, add, l2, nsend, nrecv, cin, cout, cfar, cboth, cnear,
+             sem_ld, s_nb, r_nb, s_rs, r_rs, s_ag, r_ag, s_x, r_x, s_nm, r_nm, s_e, r_e):
     v = lax.axis_index("vel")
     s = lax.axis_index("space")
     left = (v, lax.rem(s + 3, 4))
@@ -240,8 +240,6 @@
     for m in range(2):
         pbuf[m, 104:112, :] = jnp.zeros((8, CELLS), F32)
 
-    pl.semaphore_wait(barrier, PEERS - 1 + 1 + 3)
-
     def swap(i, to_right, right_dst, to_left, left_dst):
         a = pltpu.make_async_remote_copy(to_right, right_dst, s_nb.at[2 * i], r_nb.at[2 * i],
                                          device_id=right, device_id_type=MESH)
@@ -255,7 +253,6 @@
         for c in copies:
             c.wait()
 
-    halo = swap(0, rw, rwl, rw, rwr)
     settle(loads)
 
     def first(x, c):
@@ -269,6 +266,8 @@
         return c
 
     lax.fori_loop(0, X, first, 0)
+    pl.semaphore_wait(barrier, PEERS - 1 + 1 + 3)
+    halo = swap(0, rw, rwl, rw, rwr)
     edges[0, 0:16, :] = q1[1, 32:48, :]
     edges[1, 0:16, :] = q1[X, 16:32, :]
     outer1 = swap(1, edges.at[1, pl.ds(0, 16)], from_left.at[pl.ds(0, 16)],
@@ -279,7 +278,6 @@
         return c
 
     lax.fori_loop(0, X, sum_first, 0)
-    settle(halo)
 
     def alpha_row(ref, x):
         return alpha_of(ref[pl.ds(x, 1), :], ref[pl.ds(x + X, 1), :])
@@ -293,13 +291,86 @@
 
     def second(j, c):
         x = lax.rem(X - j, X)
-        val = stream_plane(dt, dhl, x + 1, x, ct, zmat, alpha_row(rw, x))
-        for i in range(LT):
-            at_[x + 2, :, 128 * i:128 * (i + 1)] = val[i]
+
+        def put(at, c, val):
+            at_[x + 2, at, c] = val
+
+        stream_plane(dt, dhl, x + 1, x, ct, zmat, zsel, put, alpha_row(rw, x))
         products(x + 1)
         return c
 
+    def third(i):
+        def put(at, c, val):
+            aa[i + 1, at, c] = val
+
+        stream_plane(at_, ahl, i + 1, i, ct, zmat, zsel, put)
+
     lax.fori_loop(0, 2, second, 0)
+    settle(outer1)
+    mine[0, 0] += from_left[0:16, :]
+    mine[0, X - 1] += from_right[0:16, :]
+
+    def pack(m):
+        for x in range(X):
+            pbuf[m, 13 * x:13 * x + 13, :] = mine[m, x, 0:13, :]
+
+    def chunk_of(o):
+        return (pl.ds(pl.multiple_of(CH * (o // LT), 8), CH), pl.ds(pl.multiple_of(128 * lax.rem(o, LT), 128), 128))
+
+    def send_parts(m):
+        def send(j, c):
+            o = lax.rem(place + j, PEERS)
+            r, k = chunk_of(o)
+            pltpu.make_async_remote_copy(pbuf.at[m, r, k], rsbuf.at[m, j], s_rs.at[m], r_rs.at[m],
+                                         device_id=peer(o), device_id_type=MESH).start()
+            return c
+
+        lax.fori_loop(1, PEERS, send, 0)
+
+    def all_parts(m):
+        return rsbuf.at[m, pl.ds(1, PEERS - 1)]
+
+    def across(m):
+        return pltpu.make_async_remote_copy(ssum.at[m], xbuf.at[m], s_x.at[m], r_x.at[m],
+                                            device_id=partner, device_id_type=MESH)
+
+    def own_sum(m):
+        pltpu.make_async_copy(all_parts(m), all_parts(m), r_rs.at[m]).wait()
+        r, k = chunk_of(place)
+        acc = pbuf[m, r, k]
+        for j in range(1, PEERS):
+            acc = acc + rsbuf[m, j]
+        ssum[m] = acc
+        across(m).start()
+
+    def send_total(m):
+        across(m).wait()
+        val = ssum[m] + xbuf[m]
+        total[m] = val
+        r, k = chunk_of(place)
+        fbuf[m, r, k] = val
+
+        def send(j, c):
+            pltpu.make_async_remote_copy(total.at[m], fbuf.at[m, r, k], s_ag.at[m], r_ag.at[m],
+                                         device_id=peer(lax.rem(place + j, PEERS)), device_id_type=MESH).start()
+            return c
+
+        lax.fori_loop(1, PEERS, send, 0)
+
+    def all_totals(m):
+        pltpu.make_async_copy(all_parts(m), all_parts(m), r_ag.at[m]).wait()
+
+    def all_sent(m):
+        pltpu.make_async_copy(all_parts(m), all_parts(m), s_rs.at[m]).wait()
+        pltpu.make_async_copy(all_parts(m), all_parts(m), s_ag.at[m]).wait()
+
+    pack(0)
+    send_parts(0)
+    lax.fori_loop(2, 7, second, 0)
+    own_sum(0)
+    lax.fori_loop(7, X, second, 0)
+
+    settle(halo)
     speed = ct[1]
     to_lower = jnp.where(speed > 0, 0.0, -speed)
     to_upper = jnp.where(speed > 0, speed, 0.0)
@@ -315,86 +386,6 @@
 
     lax.fori_loop(0, 2, ends, 0)
 
-    def third(i):
-        val = stream_plane(at_, ahl, i + 1, i, ct, zmat)
-        for t in range(LT):
-            aa[i + 1, :, 128 * t:128 * (t + 1)] = val[t]
-
-    def edge_third(j, c):
-        third((X + 1) * j)
-        return c
-
-    lax.fori_loop(0, 2, edge_third, 0)
-    for i in range(LT):
-        c = slice(128 * i, 128 * (i + 1))
-        aa[0, :, c] = to_lower * at_[1, :, c]
-        aa[X + 3, :, c] = to_upper * at_[X + 2, :, c]
-
-    settle(outer1)
-    mine[0, 0] += from_left[0:16, :]
-    mine[0, X - 1] += from_right[0:16, :]
-
-    def pack(m):
-        for x in range(X):
-            pbuf[m, 13 * x:13 * x + 13, :] = mine[m, x, 0:13, :]
-
-    def chunk_of(o):
-        return (pl.ds(pl.multiple_of(CH * (o // LT), 8), CH), pl.ds(pl.multiple_of(128 * lax.rem(o, LT), 128), 128))
-
-    def send_parts(m):
-        def send(j, c):
-            o = lax.rem(place + j, PEERS)
-            r, k = chunk_of(o)
-            pltpu.make_async_remote_copy(pbuf.at[m, r, k], rsbuf.at[m, j], s_rs.at[m], r_rs.at[m],
-                                         device_id=peer(o), device_id_type=MESH).start()
-            return c
-
-        lax.fori_loop(1, PEERS, send, 0)
-
-    def all_parts(m):
-        return rsbuf.at[m, pl.ds(1, PEERS - 1)]
-
-    def across(m):
-        return pltpu.make_async_remote_copy(ssum.at[m], xbuf.at[m], s_x.at[m], r_x.at[m],
-                                            device_id=partner, device_id_type=MESH)
-
-    def own_sum(m):
-        pltpu.make_async_copy(all_parts(m), all_parts(m), r_rs.at[m]).wait()
-        r, k = chunk_of(place)
-        acc = pbuf[m, r, k]
-        for j in range(1, PEERS):
-            acc = acc + rsbuf[m, j]
-        ssum[m] = acc
-        across(m).start()
-
-    def send_total(m):
-        across(m).wait()
-        val = ssum[m] + xbuf[m]
-        total[m] = val
-        r, k = chunk_of(place)
-        fbuf[m, r, k] = val
-
-        def send(j, c):
-            pltpu.make_async_remote_copy(total.at[m], fbuf.at[m, r, k], s_ag.at[m], r_ag.at[m],
-                                         device_id=peer(lax.rem(place + j, PEERS)), device_id_type=MESH).start()
-            return c
-
-        lax.fori_loop(1, PEERS, send, 0)
-
-    def all_totals(m):
-        pltpu.make_async_copy(all_parts(m), all_parts(m), r_ag.at[m]).wait()
-
-    def all_sent(m):
-        pltpu.make_async_copy(all_parts(m), all_parts(m), s_rs.at[m]).wait()
-        pltpu.make_async_copy(all_parts(m), all_parts(m), s_ag.at[m]).wait()
-
-    pack(0)
-    send_parts(0)
-    edge_rows = [swap(4, aa.at[X + 2], aleft.at[0], aa.at[0], aright.at[0])]
-    lax.fori_loop(2, 7, second, 0)
-    own_sum(0)
-    lax.fori_loop(7, X, second, 0)
-
     edges[0, 16:32, :] = stencil_edge(q2, 0) + q2[1, 32:48, :]
     edges[0, 32:48, :] = q2[0, 32:48, :]
     edges[1, 16:32, :] = stencil_edge(q2, X + 1) + q2[X, 16:32, :]
@@ -408,6 +399,16 @@
 
     lax.fori_loop(0, X, sum_second, 0)
     send_total(0)
+
+    def edge_third(j, c):
+        third((X + 1) * j)
+        return c
+
+    lax.fori_loop(0, 2, edge_third, 0)
+    for i in range(LT):
+        c = slice(128 * i, 128 * (i + 1))
+        aa[0, :, c] = to_lower * at_[1, :, c]
+        aa[X + 3, :, c] = to_upper * at_[X + 2, :, c]
     settle(outer2)
     mine[1, 0] += from_left[16:32, :]
     mine[1, 1] += from_left[32:48, :]
@@ -415,19 +416,41 @@
     mine[1, X - 2] += from_right[32:48, :]
     pack(1)
     send_parts(1)
-    edge_rows.append(swap(5, aa.at[X + 3], aleft.at[1], aa.at[1], aright.at[1]))
+
+    core = lax.rem(s, 2)
+    mate = (v, s + 1 - 2 * core)
+    over = (v, lax.rem(s + 2, 4))
+    half = LV // 2
+    mine_v = pl.ds(pl.multiple_of(half * core, 8), half)
+    mate_v = pl.ds(pl.multiple_of(half * (1 - core), 8), half)
+    out_end = pl.ds((X + 2) * core, 2)
+    in_end = pl.ds((X + 2) * (1 - core), 2)
+
+    def hand(i, src, dst, to):
+        c = pltpu.make_async_remote_copy(src, dst, s_e.at[i], r_e.at[i], device_id=to, device_id_type=MESH)
+        c.start()
+        return c
+
+    give = hand(0, aa.at[out_end, mate_v], cin, mate)
+    near = hand(1, aa.at[in_end], cnear, mate)
 
     def inner_third(i, c):
         third(i)
         return c
 
-    lax.fori_loop(1, X + 1, inner_third, 0)
+    lax.fori_loop(1, 3, inner_third, 0)
+    give.wait()
+    cout[...] = aa[out_end, mine_v, :] + cin[...]
+    across_x = hand(2, cout, cfar, over)
+    lax.fori_loop(3, X + 1, inner_third, 0)
     own_sum(1)
 
     all_totals(0)
     l1[...] = jnp.dot(kx[...], fbuf[0, 0:104, :], precision=HIGHEST, preferred_element_type=F32)
     halo2 = swap(3, l1.at[pl.ds(0, 64)], h_left, l1.at[pl.ds(0, 64)], h_right)
     send_total(1)
+    across_x.wait()
+    share = hand(3, cfar, cboth, mate)
     settle(halo2)
 
     zero8 = jnp.zeros((8, CELLS), F32)
@@ -491,8 +514,6 @@
         _, ylo, yhi, zlo, zhi = yz_shifts(own)
         for j, val in enumerate((ylo, yhi, zlo, zhi)):
             rhs[64 * j + 8 * k:64 * j + 8 * k + 8, :] = cat(val)
-    send_g1 = pltpu.make_async_copy(g1, g1_out, sem_out.at[0])
-    send_g1.start()
 
     def squares(l, sm):
         acc = jnp.zeros((8, CELLS), F32)
@@ -520,14 +541,25 @@
     halo3 = swap(6, b2out, b2l, b2out, b2r)
     l2[...] = jnp.dot(kx[32:208, :], m2, precision=HIGHEST, preferred_element_type=F32)
 
-    for c in edge_rows:
-        settle(c)
-    for i in range(2):
-        aa[2 + i] += aleft[i]
-    aa[X] += aright[0]
-    aa[X + 1] += aright[1]
-    send_a = pltpu.make_async_copy(aa.at[pl.ds(2, X)], a_out, sem_out.at[1])
-    send_a.start()
+    near.wait()
+    share.wait()
+    is_upper = (core == 0).astype(F32)
+    from_far = 2 + (X - 2) * core
+    from_near = 2 + (X - 2) * (1 - core)
+
+    def add_ends(i, carry):
+        for t in range(LT):
+            c = slice(128 * t, 128 * (t + 1))
+            aa[from_near + i, :, c] += cnear[i, :, c]
+            aa[from_far + i, mine_v, c] += jnp.where(wanted_of(mine_v) > 0, cfar[i, :, c], 0.0)
+            aa[from_far + i, mate_v, c] += jnp.where(wanted_of(mate_v) > 0, cboth[i, :, c], 0.0)
+        return carry
+
+    def wanted_of(rows):
+        towards = ct[1, rows, :]
+        return jnp.where(towards > 0, is_upper, 1.0 - is_upper)
+
+    lax.fori_loop(0, 2, add_ends, 0)
 
     settle(halo3)
     for k in range(4):
@@ -573,8 +605,6 @@
     settle(notes)
     for i in range(2):
         norm_out[i] = (nsend[i] + nrecv[0, i]) + (nrecv[1, i] + nrecv[2, i])
-    send_g1.wait()
-    send_a.wait()
     for m in range(2):
         all_sent(m)
 
@@ -594,13 +624,8 @@
 PAIRS = 4
 
 
-def renew(a_hbm, g1_ref, g2_ref, relax_ref, wall_ref, vel_ref, mac_ref, sum_ref, out_hbm, mac_out, norm_out,
-          abuf, obuf, stage, rhs, lt, lrows, sem_in, sem_out):
-    fetch = [
-        pltpu.make_async_copy(a_hbm.at[:, :, pl.ds(256 * i, 256)], abuf.at[i], sem_in.at[i]) for i in range(PAIRS)
-    ]
-    for c in fetch:
-        c.start()
+def renew(a_ref, g1_ref, g2_ref, relax_ref, wall_ref, vel_ref, mac_ref, sum_ref, out_hbm, mac_out, norm_out,
+          obuf, stage, rhs, lt, lrows, sem_out):
     mac_out[...] = mac_ref[...]
     for i in range(2):
         norm_out[i] = jnp.sqrt(jnp.sum(sum_ref[i]))
@@ -643,11 +668,9 @@
 
     puts = []
     for i in range(PAIRS):
-        fetch[i].wait()
-
         def plane(x, c):
             al = alpha_of(relax_ref[pl.ds(x, 1), 256 * i:256 * (i + 1)], wall_ref[pl.ds(x, 1), 256 * i:256 * (i + 1)])
-            val = jnp.dot(lt[...], rhs[x, :, 256 * i:256 * (i + 1)], preferred_element_type=F32) + al * abuf[i, x]
+            val = jnp.dot(lt[...], rhs[x, :, 256 * i:256 * (i + 1)], preferred_element_type=F32) + al * a_ref[x + 2, :, 256 * i:256 * (i + 1)]
             obuf[2 * i, pl.ds(x, LV, stride=X), :] = val[:, 0:128]
             obuf[2 * i + 1, pl.ds(x, LV, stride=X), :] = val[:, 128:256]
             return c
@@ -670,16 +693,16 @@
     a, g1, g2, mac, norm = pl.pallas_call(
         exchange,
         out_shape=(
-            sds((X, LV, CELLS), F32), sds((8 * EXT, CELLS), F32), sds((64, CELLS), F32),
-            sds((MOM, X, 32), F32), sds((2, 8, 128), F32),
+            pltpu.VMEM((X + 4, LV, CELLS), F32), pltpu.VMEM((8 * EXT, CELLS), F32), pltpu.VMEM((64, CELLS), F32),
+            pltpu.VMEM((MOM, X, 32), F32), pltpu.VMEM((2, 8, 128), F32),
         ),
         in_specs=[hbm] + [vmem] * 9,
-        out_specs=(hbm, hbm, vmem, vmem, vmem),
+        out_specs=(vmem,) * 5,
         scratch_shapes=[
             pltpu.VMEM((LT, LV * X, 128), F32),
             pltpu.VMEM((X + 2, LV, CELLS), F32),
             pltpu.VMEM((X + 4, LV, CELLS), F32),
-            pltpu.VMEM((X + 4, LV, CELLS), F32),
+            pltpu.VMEM((LV, CELLS), F32),
             pltpu.VMEM((X, 2 * LV, CELLS), BF16),
             pltpu.VMEM((X + 2, 2 * LV, CELLS), BF16),
             pltpu.VMEM((X + 2, 112, CELLS), F32),
@@ -710,36 +733,37 @@
             pltpu.VMEM((32, CELLS), F32),
             pltpu.VMEM((2, 4, 32, CELLS), F32),
             pltpu.VMEM((4, EXT, CELLS), F32),
-            pltpu.VMEM((8 * EXT, CELLS), F32),
             pltpu.VMEM((256, CELLS), F32),
             pltpu.VMEM((X * MOM, CELLS), F32),
             pltpu.VMEM((22 * X, CELLS), F32),
             pltpu.VMEM((2, 8, 128), F32),
             pltpu.VMEM((3, 2, 8, 128), F32),
-            pltpu.VMEM((2, LV, CELLS), F32),
+            pltpu.VMEM((2, LV // 2, CELLS), F32),
+            pltpu.VMEM((2, LV // 2, CELLS), F32),
+            pltpu.VMEM((2, LV // 2, CELLS), F32),
+            pltpu.VMEM((2, LV // 2, CELLS), F32),
             pltpu.VMEM((2, LV, CELLS), F32),
             dma((LT,)), dma((14,)), dma((14,)), dma((2,)), dma((2,)), dma((2,)), dma((2,)), dma((2,)), dma((2,)),
-            dma((3,)), dma((3,)), dma((2,)),
+            dma((3,)), dma((3,)), dma((4,)), dma((4,)),
         ],
-        compiler_params=pltpu.CompilerParams(collective_id=0, has_side_effects=True, vmem_limit_bytes=60 * 2 ** 20),
+        compiler_params=pltpu.CompilerParams(collective_id=0, has_side_effects=True, vmem_limit_bytes=54 * 2 ** 20),
         name="exchange",
     )(dist.reshape(LV * X, CELLS), relax, wall_mask, vel_index, macro_inverse, *consts)
 
     out, mac, norm = pl.pallas_call(
         renew,
         out_shape=(sds((LV * X, CELLS), F32), sds((MOM, X, 32), F32), sds((2,), F32)),
-        in_specs=[hbm] + [vmem] * 7,
+        in_specs=[vmem] * 8,
         out_specs=(hbm, vmem, smem),
         scratch_shapes=[
-            pltpu.VMEM((PAIRS, X, LV, 256), F32),
             pltpu.VMEM((LT, LV * X, 128), F32),
             pltpu.VMEM((LT, 512, 128), F32),
             pltpu.VMEM((X, 256, CELLS), BF16),
             pltpu.VMEM((LV, 256), BF16),
             pltpu.VMEM((64, LV), F32),
-            dma((PAIRS,)), dma((LT,)),
+            dma((LT,)),
         ],
-        compiler_params=pltpu.CompilerParams(vmem_limit_bytes=60 * 2 ** 20),
+        compiler_params=pltpu.CompilerParams(vmem_limit_bytes=32 * 2 ** 20),
         name="renew",
     )(a, g1, g2, relax, wall_mask, vel_index, mac, norm)
     return (out.reshape(LV, X, CELLS), mac, norm)

time: 78.8 us -> 75.6 us (0.959)
  Pallas kernels: 78 us -> 74.8 us
    pallas_call x1, Pallas kernels: 67.4 us -> 65.4 us  [shards(): pl.pallas_call(exchange, out_shape=(pltpu.VMEM((X + 4, LV, CELLS), F32),...]
    pallas_call x1, Pallas kernels: 10.6 us -> 9.31 us  [shards(): pl.pallas_call(renew, out_shape=(sds((LV * X, CELLS), F32), sds((MOM, X,...]
where the time goes in v3:
time: 75.6 us; the launch traced here: 75.5 us
  Pallas kernels  74.8 us (99%)
    pallas_call x1, Pallas kernels, shards(): pl.pallas_call(exchange, out_shape=(pltpu.VMEM((X + 4, LV, CELLS), F32),...  65.4 us
    pallas_call x1, Pallas kernels, shards(): pl.pallas_call(renew, out_shape=(sds((LV * X, CELLS), F32), sds((MOM, X,...  9.31 us

profile of v3, /device:TPU:1, one launch (start us, length us, event | category | flops | bytes accessed | tf_op | source)
XLA Modules:
  0.0 75.5 jit_solution(2616382919143687040)
XLA Ops:
  0.6 0.0 copy-start.1
  0.6 0.0 copy-start
  0.7 0.0 copy-start.2
  0.7 65.4 %exchange.1 = (f32[12,128,1024]{2,1,0:T(8,128)S(1)}, f32[128,1024]{1,0:T(8,128)S(1)}, f32[64,1024]{1,0:T(8,128)S(1)}, f32[13,8,32]{2,1,0:T(8,128)S(1)}, f32[2,8,128]{2,1,0:T(8,128)S(1)}) custom-call(f32[1024,1024]{1,0:T(8,128)} %bitcast.2, f32[8,1024]{1,0:T(8,128)} %relax_ref.3, s32[8,1024]{1,0:T(8,128)} %wall_ref.3, s32[3,128]{1,0:T(4,128)} %vel_ref.3, ...), custom_call_target="tpu_custom_call" | custom-call | tf_op jit(solution)/shard_map/exchange/pallas_call | solution.py:693
  66.1 0.0 copy-done.1
  66.1 0.0 copy-done
  66.1 0.0 copy-done.2
  66.1 9.3 %renew.1 = (f32[1024,1024]{1,0:T(8,128)}, f32[13,8,32]{2,1,0:T(8,128)}, f32[2]{0:T(128)}) custom-call(f32[12,128,1024]{2,1,0:T(8,128)S(1)} %get-tuple-element.11.a_ref, f32[128,1024]{1,0:T(8,128)S(1)} %get-tuple-element.12.g1_ref, f32[64,1024]{1,0:T(8,128)S(1)} %get-tuple-element.13.g2_ref, f32[8,1024]{1,0:T(8,128)S(1)} %copy-done, s32[8,1024]{1,0:T(8,128)S(1)} %copy-done.1, ...), custom_call_target="tpu_custom_call" | custom-call | tf_op jit(solution)/shard_map/renew/pallas_call | solution.py:753
Async XLA Ops:
  0.6 65.5 %copy-start.1 = (s32[8,1024]{1,0:T(8,128)S(1)}, s32[8,1024]{1,0:T(8,128)}, u32[]{:S(2)}) copy-start(s32[8,1024]{1,0:T(8,128)} %wall_ref.3) | copy-start | bytes 98308
  0.6 65.5 %copy-start = (f32[8,1024]{1,0:T(8,128)S(1)}, f32[8,1024]{1,0:T(8,128)}, u32[]{:S(2)}) copy-start(f32[8,1024]{1,0:T(8,128)} %relax_ref.3) | copy-start | bytes 98308
  0.7 65.5 %copy-start.2 = (s32[3,128]{1,0:T(4,128)S(1)}, s32[3,128]{1,0:T(4,128)}, u32[]{:S(2)}) copy-start(s32[3,128]{1,0:T(4,128)} %vel_ref.3) | copy-start | bytes 4612

commit v4 on v3

--- a/solution.py
+++ b/solution.py
@@ -141,40 +141,40 @@
     return jnp.where(wall > 0, 0.0, 1.0 - relax)
 
 
-def stream_plane(src, halves, p, h, ct, zmat, zsel, put, scale=None):
-    pz = ct[3] > 0
+def stream_plane(src, halves, p, h, ct, zmat, scale=None):
+    lane = lax.broadcasted_iota(jnp.int32, (LV, 128), 1)
+    k0, cx, cy, cz = (ct[i] for i in range(4))
+    px, py, pz = cx > 0, cy > 0, cz > 0
+    kx, ky, kz = jnp.abs(cx), jnp.abs(cy), jnp.abs(cz)
+    t = [src[p, :, 128 * i:128 * (i + 1)] for i in range(LT)]
+    z = [
+        jnp.dot(
+            cat([halves[h, 0:LV, 128 * i:128 * (i + 1)], halves[h, LV:2 * LV, 128 * i:128 * (i + 1)]]),
+            zmat[...],
+            preferred_element_type=F32,
+        )
+        for i in range(LT)
+    ]
+    up = [pltpu.roll(a, 16, 1) for a in t]
+    down = [pltpu.roll(a, 112, 1) for a in t]
+    out = []
     for i in range(LT):
-        c = slice(128 * i, 128 * (i + 1))
-        z = jnp.dot(cat([halves[h, 0:LV, c], halves[h, LV:2 * LV, c]]), zmat[...], preferred_element_type=F32)
-        zsel[:, c] = jnp.where(pz, z[:, 0:128], z[:, 128:256])
-
-    def group(g, carry):
-        at = pl.ds(pl.multiple_of(8 * g, 8), 8)
-        lane = lax.broadcasted_iota(jnp.int32, (8, 128), 1)
-        k0, cx, cy, cz = (ct[i, at, :] for i in range(4))
-        px, py = cx > 0, cy > 0
-        kx, ky, kz = jnp.abs(cx), jnp.abs(cy), jnp.abs(cz)
-        t = [src[p, at, 128 * i:128 * (i + 1)] for i in range(LT)]
-        up = [pltpu.roll(a, 16, 1) for a in t]
-        down = [pltpu.roll(a, 112, 1) for a in t]
-        for i in range(LT):
-            c = slice(128 * i, 128 * (i + 1))
-            in_x = jnp.where(px, src[p - 1, at, c], src[p + 1, at, c])
-            in_y = jnp.where(
-                py,
-                jnp.where(lane < 16, up[i - 1], up[i]),
-                jnp.where(lane >= 112, down[(i + 1) % LT], down[i]),
-            )
-            val = (k0 * t[i] + kx * in_x) + (ky * in_y + kz * zsel[at, c])
-            put(at, c, val if scale is None else val * scale[:, c])
-        return carry
-
-    lax.fori_loop(0, LV // 8, group, 0, unroll=4)
+        s = slice(128 * i, 128 * (i + 1))
+        in_x = jnp.where(px, src[p - 1, :, s], src[p + 1, :, s])
+        in_y = jnp.where(
+            py,
+            jnp.where(lane < 16, up[i - 1], up[i]),
+            jnp.where(lane >= 112, down[(i + 1) % LT], down[i]),
+        )
+        in_z = jnp.where(pz, z[i][:, 0:128], z[i][:, 128:256])
+        val = (k0 * t[i] + kx * in_x) + (ky * in_y + kz * in_z)
+        out.append(val if scale is None else val * scale[:, s])
+    return out
 
 
 def exchange(dist_hbm, relax_ref, wall_ref, vel_ref, inv_ref, sel_ref, spread_ref, mask_ref, fixed_ref, nc,
              aa, g1, g2_out, mac_out, norm_out,
-             dbuf, dt, at_, zsel, dhl, ahl, q1, q2, mine, edges, from_left, from_right, rw, rwl, rwr,
+             dbuf, dt, at_, dhl, ahl, q1, q2, mine, edges, from_left, from_right, rw, rwl, rwr,
              mrows, lm, ct, zmat, kx, pbuf, rsbuf, ssum, xbuf, total, fbuf, l1, h_left, h_right, b2out, b2l, b2r,
              u, b, rhs, add, l2, nsend, nrecv, cin, cout, cfar, cboth, cnear,
              sem_ld, s_nb, r_nb, s_rs, r_rs, s_ag, r_ag, s_x, r_x, s_nm, r_nm, s_e, r_e):
@@ -292,18 +292,16 @@
     def second(j, c):
         x = lax.rem(X - j, X)
 
-        def put(at, c, val):
-            at_[x + 2, at, c] = val
-
-        stream_plane(dt, dhl, x + 1, x, ct, zmat, zsel, put, alpha_row(rw, x))
+        val = stream_plane(dt, dhl, x + 1, x, ct, zmat, alpha_row(rw, x))
+        for i in range(LT):
+            at_[x + 2, :, 128 * i:128 * (i + 1)] = val[i]
         products(x + 1)
         return c
 
     def third(i):
-        def put(at, c, val):
-            aa[i + 1, at, c] = val
-
-        stream_plane(at_, ahl, i + 1, i, ct, zmat, zsel, put)
+        val = stream_plane(at_, ahl, i + 1, i, ct, zmat)
+        for t in range(LT):
+            aa[i + 1, :, 128 * t:128 * (t + 1)] = val[t]
 
     lax.fori_loop(0, 2, second, 0)
     settle(outer1)
@@ -449,8 +447,6 @@
     l1[...] = jnp.dot(kx[...], fbuf[0, 0:104, :], precision=HIGHEST, preferred_element_type=F32)
     halo2 = swap(3, l1.at[pl.ds(0, 64)], h_left, l1.at[pl.ds(0, 64)], h_right)
     send_total(1)
-    across_x.wait()
-    share = hand(3, cfar, cboth, mate)
     settle(halo2)
 
     zero8 = jnp.zeros((8, CELLS), F32)
@@ -535,6 +531,8 @@
         jnp.dot(nc[:, 0:128], g1[...], precision=HIGHEST, preferred_element_type=F32)
         + jnp.dot(nc[:, 128:384], rhs[...], precision=HIGHEST, preferred_element_type=F32)
     )
+    across_x.wait()
+    share = hand(3, cfar, cboth, mate)
     all_totals(1)
     m2 = fbuf[1, 0:104, :] + add[...]
     b2out[...] = jnp.dot(kx[0:32, :], m2, precision=HIGHEST, preferred_element_type=F32)
@@ -702,7 +700,6 @@
             pltpu.VMEM((LT, LV * X, 128), F32),
             pltpu.VMEM((X + 2, LV, CELLS), F32),
             pltpu.VMEM((X + 4, LV, CELLS), F32),
-            pltpu.VMEM((LV, CELLS), F32),
             pltpu.VMEM((X, 2 * LV, CELLS), BF16),
             pltpu.VMEM((X + 2, 2 * LV, CELLS), BF16),
             pltpu.VMEM((X + 2, 112, CELLS), F32),

time: 75.6 us -> 74.7 us (0.988)
  Pallas kernels: 74.8 us -> 73.9 us
    pallas_call x1, Pallas kernels: 65.4 us -> 64.6 us  [shards(): pl.pallas_call(exchange, out_shape=(pltpu.VMEM((X + 4, LV, CELLS), F32),...]
where the time goes in v4:
time: 74.7 us; the launch traced here: 74.6 us
  Pallas kernels  73.9 us (99%)
    pallas_call x1, Pallas kernels, shards(): pl.pallas_call(exchange, out_shape=(pltpu.VMEM((X + 4, LV, CELLS), F32),...  64.6 us
    pallas_call x1, Pallas kernels, shards(): pl.pallas_call(renew, out_shape=(sds((LV * X, CELLS), F32), sds((MOM, X,...  9.31 us

profile of v4, /device:TPU:1, one launch (start us, length us, event | category | flops | bytes accessed | tf_op | source)
XLA Modules:
  0.0 74.6 jit_solution(4823510318189925778)
XLA Ops:
  0.6 0.0 copy-start.1
  0.6 0.0 copy-start
  0.7 0.0 copy-start.2
  0.7 64.6 %exchange.1 = (f32[12,128,1024]{2,1,0:T(8,128)S(1)}, f32[128,1024]{1,0:T(8,128)S(1)}, f32[64,1024]{1,0:T(8,128)S(1)}, f32[13,8,32]{2,1,0:T(8,128)S(1)}, f32[2,8,128]{2,1,0:T(8,128)S(1)}) custom-call(f32[1024,1024]{1,0:T(8,128)} %bitcast.2, f32[8,1024]{1,0:T(8,128)} %relax_ref.3, s32[8,1024]{1,0:T(8,128)} %wall_ref.3, s32[3,128]{1,0:T(4,128)} %vel_ref.3, ...), custom_call_target="tpu_custom_call" | custom-call | tf_op jit(solution)/shard_map/exchange/pallas_call | solution.py:691
  65.2 0.0 copy-done.1
  65.2 0.0 copy-done
  65.2 0.0 copy-done.2
  65.2 9.3 %renew.1 = (f32[1024,1024]{1,0:T(8,128)}, f32[13,8,32]{2,1,0:T(8,128)}, f32[2]{0:T(128)}) custom-call(f32[12,128,1024]{2,1,0:T(8,128)S(1)} %get-tuple-element.11.a_ref, f32[128,1024]{1,0:T(8,128)S(1)} %get-tuple-element.12.g1_ref, f32[64,1024]{1,0:T(8,128)S(1)} %get-tuple-element.13.g2_ref, f32[8,1024]{1,0:T(8,128)S(1)} %copy-done, s32[8,1024]{1,0:T(8,128)S(1)} %copy-done.1, ...), custom_call_target="tpu_custom_call" | custom-call | tf_op jit(solution)/shard_map/renew/pallas_call | solution.py:750
Async XLA Ops:
  0.6 64.6 %copy-start.1 = (s32[8,1024]{1,0:T(8,128)S(1)}, s32[8,1024]{1,0:T(8,128)}, u32[]{:S(2)}) copy-start(s32[8,1024]{1,0:T(8,128)} %wall_ref.3) | copy-start | bytes 98308
  0.6 64.6 %copy-start = (f32[8,1024]{1,0:T(8,128)S(1)}, f32[8,1024]{1,0:T(8,128)}, u32[]{:S(2)}) copy-start(f32[8,1024]{1,0:T(8,128)} %relax_ref.3) | copy-start | bytes 98308
  0.7 64.6 %copy-start.2 = (s32[3,128]{1,0:T(4,128)S(1)}, s32[3,128]{1,0:T(4,128)}, u32[]{:S(2)}) copy-start(s32[3,128]{1,0:T(4,128)} %vel_ref.3) | copy-start | bytes 4612

commit v5 on v4

--- a/solution.py
+++ b/solution.py
@@ -173,10 +173,10 @@
 
 
 def exchange(dist_hbm, relax_ref, wall_ref, vel_ref, inv_ref, sel_ref, spread_ref, mask_ref, fixed_ref, nc,
-             aa, g1, g2_out, mac_out, norm_out,
+             aa, g2_out, mac_out, norm_out,
              dbuf, dt, at_, dhl, ahl, q1, q2, mine, edges, from_left, from_right, rw, rwl, rwr,
-             mrows, lm, ct, zmat, kx, pbuf, rsbuf, ssum, xbuf, total, fbuf, l1, h_left, h_right, b2out, b2l, b2r,
-             u, b, rhs, add, l2, nsend, nrecv, cin, cout, cfar, cboth, cnear,
+             mrows, lm, ct, zmat, kx, pbuf, rsbuf, ssum, xbuf, total, fbuf, l1, h_out, h_left, h_right, b2out, b2_out, b2l, b2r,
+             u, b, g1, rhs, lrows, lt, add, l2, nsend, nrecv, cin, cout, cfar, cboth, cnear,
              sem_ld, s_nb, r_nb, s_rs, r_rs, s_ag, r_ag, s_x, r_x, s_nm, r_nm, s_e, r_e):
     v = lax.axis_index("vel")
     s = lax.axis_index("space")
@@ -208,7 +208,7 @@
     rw[X:2 * X, :] = wall_ref[...].astype(F32)
     vel = speed_range * (2.0 * vel_ref[...].astype(F32) + 1.0 - NVX) / NVX
     cx, cy, cz = vel[0:1], vel[1:2], vel[2:3]
-    rows, _, stencil = functions_of(cx, cy, cz)
+    rows, target, stencil = functions_of(cx, cy, cz)
     mrows[...] = jnp.zeros_like(mrows)
     for r in range(MOM):
         mrows[r:r + 1, :] = rows[r]
@@ -220,6 +220,14 @@
         lm[112 + 16 * o:128 + 16 * o, LV:2 * LV] = jnp.zeros_like(lo)
     for i, row in enumerate((stencil[0], time_step * cx, time_step * cy, time_step * cz)):
         ct[i] = jnp.transpose(jnp.broadcast_to(row, (LV, LV)))
+    for k in range(8):
+        for o in range(7):
+            lrows[8 * o + k:8 * o + k + 1, :] = stencil[o] * target[k]
+    hi, lo = split(lrows[...])
+    hi, lo = hi.astype(F32), lo.astype(F32)
+    quad = jnp.concatenate([hi, hi, lo, lo, jnp.zeros((32, LV), F32)], 0)
+    lt[:, 0:128] = jnp.transpose(quad[0:128]).astype(BF16)
+    lt[:, 128:224] = jnp.transpose(quad[128:256])[:, 0:96].astype(BF16)
     src_lane = lax.broadcasted_iota(jnp.int32, (LV, LV), 0)
     dst_lane = lax.broadcasted_iota(jnp.int32, (LV, LV), 1)
     dst_z = dst_lane % NZ
@@ -364,9 +372,7 @@
 
     pack(0)
     send_parts(0)
-    lax.fori_loop(2, 7, second, 0)
-    own_sum(0)
-    lax.fori_loop(7, X, second, 0)
+    lax.fori_loop(2, X, second, 0)
 
     settle(halo)
     speed = ct[1]
@@ -390,13 +396,13 @@
     edges[1, 32:48, :] = q2[X + 1, 16:32, :]
     outer2 = swap(2, edges.at[1, pl.ds(16, 32)], from_left.at[pl.ds(16, 32)],
                   edges.at[0, pl.ds(16, 32)], from_right.at[pl.ds(16, 32)])
+    own_sum(0)
 
     def sum_second(x, c):
         mine[1, x] = stencil_moments(q2, x + 1)
         return c
 
     lax.fori_loop(0, X, sum_second, 0)
-    send_total(0)
 
     def edge_third(j, c):
         third((X + 1) * j)
@@ -414,6 +420,7 @@
     mine[1, X - 2] += from_right[32:48, :]
     pack(1)
     send_parts(1)
+    send_total(0)
 
     core = lax.rem(s, 2)
     mate = (v, s + 1 - 2 * core)
@@ -439,14 +446,19 @@
     lax.fori_loop(1, 3, inner_third, 0)
     give.wait()
     cout[...] = aa[out_end, mine_v, :] + cin[...]
-    across_x = hand(2, cout, cfar, over)
-    lax.fori_loop(3, X + 1, inner_third, 0)
-    own_sum(1)
+    over_0 = hand(2, cout.at[0], cfar.at[0], over)
+    lax.fori_loop(3, 6, inner_third, 0)
 
     all_totals(0)
     l1[...] = jnp.dot(kx[...], fbuf[0, 0:104, :], precision=HIGHEST, preferred_element_type=F32)
-    halo2 = swap(3, l1.at[pl.ds(0, 64)], h_left, l1.at[pl.ds(0, 64)], h_right)
+    for k in range(8):
+        h_out[0, HALO * k:HALO * (k + 1), :] = l1[8 * k:8 * k + HALO, :]
+        h_out[1, HALO * k:HALO * (k + 1), :] = l1[8 * k + X - HALO:8 * k + X, :]
+    halo2 = swap(3, h_out.at[1], h_left, h_out.at[0], h_right)
+    own_sum(1)
+    lax.fori_loop(6, X + 1, inner_third, 0)
     send_total(1)
+    over_1 = hand(3, cout.at[1], cfar.at[1], over)
     settle(halo2)
 
     zero8 = jnp.zeros((8, CELLS), F32)
@@ -486,12 +498,13 @@
         return SWEEPS % 2
 
     for k in range(4):
-        fill(k, h_left[8 * k + 4:8 * k + 8, :], l1[8 * k:8 * k + 8, :], h_right[8 * k:8 * k + 4, :])
+        fill(k, h_left[4 * k:4 * k + 4, :], l1[8 * k:8 * k + 8, :], h_right[4 * k:4 * k + 4, :])
     last = smooth()
 
     def gammas(relax, wall):
         return jnp.where(wall > 0, 0.0, relax), jnp.where(wall > 0, 1.0, relax)
 
+    own_alpha = alpha_of(rw[0:X, :], rw[X:2 * X, :])
     factors = [gammas(ref[0:X, :], ref[X:2 * X, :]) for ref in (rwl, rw, rwr)]
     for k in range(8):
         gl, go, gr = (f[1 if k in (3, 4) else 0] for f in factors)
@@ -500,16 +513,23 @@
             own = u[last, k, 8 + HALO:8 + HALO + X, :]
             hi_rows = u[last, k, 8 + HALO + X:8 + EXT, :]
         else:
-            lo_rows = h_left[8 * k + 4:8 * k + 8, :]
+            lo_rows = h_left[4 * k:4 * k + 4, :]
             own = l1[8 * k:8 * k + 8, :]
-            hi_rows = h_right[8 * k:8 * k + 4, :]
+            hi_rows = h_right[4 * k:4 * k + 4, :]
         own = own * go
         g1[EXT * k:EXT * k + HALO, :] = lo_rows * gl[4:8]
         g1[EXT * k + HALO:EXT * k + HALO + X, :] = own
         g1[EXT * k + HALO + X:EXT * (k + 1), :] = hi_rows * gr[0:4]
-        _, ylo, yhi, zlo, zhi = yz_shifts(own)
+        here, ylo, yhi, zlo, zhi = yz_shifts(own)
         for j, val in enumerate((ylo, yhi, zlo, zhi)):
             rhs[64 * j + 8 * k:64 * j + 8 * k + 8, :] = cat(val)
+        at = EXT * k + HALO
+        before = tiles(g1[at - 1:at + 7, :])
+        after = tiles(g1[at + 1:at + 9, :])
+        for t in range(LT):
+            al = own_alpha[:, 128 * t:128 * (t + 1)]
+            for o, val in enumerate((here, before, after, ylo, yhi, zlo, zhi)):
+                dbuf[t, 64 * o + 8 * k:64 * o + 8 * k + 8, :] = val[t] * al
 
     def squares(l, sm):
         acc = jnp.zeros((8, CELLS), F32)
@@ -531,37 +551,40 @@
         jnp.dot(nc[:, 0:128], g1[...], precision=HIGHEST, preferred_element_type=F32)
         + jnp.dot(nc[:, 128:384], rhs[...], precision=HIGHEST, preferred_element_type=F32)
     )
-    across_x.wait()
-    share = hand(3, cfar, cboth, mate)
+
+    def spread(x, c):
+        for t in range(LT):
+            hi, lo = split(dbuf[t, pl.ds(x, 56, stride=X), :])
+            both_parts = jnp.concatenate([hi.astype(F32), lo.astype(F32)], 0).astype(BF16)
+            cols = slice(128 * t, 128 * (t + 1))
+            dhl[x, 0:112, cols] = both_parts
+            dhl[x, 112:224, cols] = both_parts
+        return c
+
+    lax.fori_loop(0, X, spread, 0)
+    over_0.wait()
+    over_1.wait()
+    share = hand(4, cfar, cboth, mate)
     all_totals(1)
     m2 = fbuf[1, 0:104, :] + add[...]
     b2out[...] = jnp.dot(kx[0:32, :], m2, precision=HIGHEST, preferred_element_type=F32)
-    halo3 = swap(6, b2out, b2l, b2out, b2r)
+    for k in range(4):
+        b2_out[0, HALO * k:HALO * (k + 1), :] = b2out[8 * k:8 * k + HALO, :]
+        b2_out[1, HALO * k:HALO * (k + 1), :] = b2out[8 * k + X - HALO:8 * k + X, :]
+    halo3 = swap(6, b2_out.at[1], b2l, b2_out.at[0], b2r)
     l2[...] = jnp.dot(kx[32:208, :], m2, precision=HIGHEST, preferred_element_type=F32)
 
-    near.wait()
-    share.wait()
-    is_upper = (core == 0).astype(F32)
-    from_far = 2 + (X - 2) * core
-    from_near = 2 + (X - 2) * (1 - core)
-
-    def add_ends(i, carry):
-        for t in range(LT):
-            c = slice(128 * t, 128 * (t + 1))
-            aa[from_near + i, :, c] += cnear[i, :, c]
-            aa[from_far + i, mine_v, c] += jnp.where(wanted_of(mine_v) > 0, cfar[i, :, c], 0.0)
-            aa[from_far + i, mate_v, c] += jnp.where(wanted_of(mate_v) > 0, cboth[i, :, c], 0.0)
-        return carry
-
-    def wanted_of(rows):
-        towards = ct[1, rows, :]
-        return jnp.where(towards > 0, is_upper, 1.0 - is_upper)
-
-    lax.fori_loop(0, 2, add_ends, 0)
-
+    def combine(x):
+        aa[x + 2] = jnp.dot(lt[...], dhl[x, 0:224, :], preferred_element_type=F32) + alpha_row(rw, x) * aa[x + 2]
+
+    def middle(x, c):
+        combine(x)
+        return c
+
+    lax.fori_loop(2, X - 2, middle, 0)
     settle(halo3)
     for k in range(4):
-        fill(k, b2l[8 * k + 4:8 * k + 8, :], b2out[8 * k:8 * k + 8, :], b2r[8 * k:8 * k + 4, :])
+        fill(k, b2l[4 * k:4 * k + 4, :], b2out[8 * k:8 * k + 8, :], b2r[4 * k:4 * k + 4, :])
     last = smooth()
     acc = jnp.zeros((8, CELLS), F32)
     for i in range(9):
@@ -600,6 +623,32 @@
             f = l2[136 + 8 * (r - 5):144 + 8 * (r - 5), tile]
         mac_out[r] = pltpu.roll(f, turn, 1)[:, 0:32]
 
+    near.wait()
+    share.wait()
+    is_upper = (core == 0).astype(F32)
+    from_far = 2 + (X - 2) * core
+    from_near = 2 + (X - 2) * (1 - core)
+
+    def add_ends(i, carry):
+        for t in range(LT):
+            c = slice(128 * t, 128 * (t + 1))
+            aa[from_near + i, :, c] += cnear[i, :, c]
+            aa[from_far + i, mine_v, c] += jnp.where(wanted_of(mine_v) > 0, cfar[i, :, c], 0.0)
+            aa[from_far + i, mate_v, c] += jnp.where(wanted_of(mate_v) > 0, cboth[i, :, c], 0.0)
+        return carry
+
+    def wanted_of(rows):
+        towards = ct[1, rows, :]
+        return jnp.where(towards > 0, is_upper, 1.0 - is_upper)
+
+    lax.fori_loop(0, 2, add_ends, 0)
+
+    def outside(j, c):
+        combine(lax.rem(j + X - 2, X))
+        return c
+
+    lax.fori_loop(0, 4, outside, 0)
+
     settle(notes)
     for i in range(2):
         norm_out[i] = (nsend[i] + nrecv[0, i]) + (nrecv[1, i] + nrecv[2, i])
@@ -622,53 +671,40 @@
 PAIRS = 4
 
 
-def renew(a_ref, g1_ref, g2_ref, relax_ref, wall_ref, vel_ref, mac_ref, sum_ref, out_hbm, mac_out, norm_out,
-          obuf, stage, rhs, lt, lrows, sem_out):
+def renew(a_ref, g2_ref, vel_ref, mac_ref, sum_ref, out_hbm, mac_out, norm_out, obuf, stage, rhs, lt, sem_out):
     mac_out[...] = mac_ref[...]
     for i in range(2):
         norm_out[i] = jnp.sqrt(jnp.sum(sum_ref[i]))
-    alpha = alpha_of(relax_ref[...], wall_ref[...])
 
     vel = speed_range * (2.0 * vel_ref[...].astype(F32) + 1.0 - NVX) / NVX
-    _, target, stencil = functions_of(vel[0:1], vel[1:2], vel[2:3])
+    _, target, _ = functions_of(vel[0:1], vel[1:2], vel[2:3])
     for k in range(8):
-        for o in range(7):
-            lrows[8 * o + k:8 * o + k + 1, :] = stencil[o] * target[k]
-        lrows[56 + k:57 + k, :] = target[k]
-    hi, lo = split(lrows[...])
+        stage[0, k:k + 1, :] = target[k]
+    hi, lo = split(stage[0, 0:8, :])
     hi, lo = hi.astype(F32), lo.astype(F32)
-    lt[:, 0:128] = jnp.transpose(jnp.concatenate([hi, hi], 0)).astype(BF16)
-    lt[:, 128:256] = jnp.transpose(jnp.concatenate([lo, lo], 0)).astype(BF16)
-
-    for k in range(8):
-        at = EXT * k + HALO
-        here, ylo, yhi, zlo, zhi = yz_shifts(g1_ref[at:at + 8, :])
-        before = g1_ref[at - 1:at + 7, :]
-        after = g1_ref[at + 1:at + 9, :]
-        for t in range(LT):
-            cols = slice(128 * t, 128 * (t + 1))
-            vals = (here[t], before[:, cols], after[:, cols], ylo[t], yhi[t], zlo[t], zhi[t])
-            for o, val in enumerate(vals):
-                stage[t, 64 * o + 8 * k:64 * o + 8 * k + 8, :] = val * alpha[:, cols]
-            stage[t, 448 + 8 * k:456 + 8 * k, :] = g2_ref[8 * k:8 * k + 8, cols]
+    quad = jnp.concatenate([hi, hi, lo, lo, jnp.zeros((96, LV), F32)], 0)
+    lt[...] = jnp.transpose(quad)[:, 0:32].astype(BF16)
+
+    for t in range(LT):
+        stage[t] = g2_ref[:, 128 * t:128 * (t + 1)]
 
     def spread(x, c):
         for t in range(LT):
-            hi, lo = split(stage[t, pl.ds(x, 64, stride=X), :])
+            hi, lo = split(stage[t, pl.ds(x, 8, stride=X), :])
+            both_parts = jnp.concatenate([hi.astype(F32), lo.astype(F32)], 0).astype(BF16)
             cols = slice(128 * t, 128 * (t + 1))
-            rhs[x, 0:64, cols] = hi
-            rhs[x, 64:128, cols] = lo
-            rhs[x, 128:192, cols] = hi
-            rhs[x, 192:256, cols] = lo
+            rhs[x, 0:16, cols] = both_parts
+            rhs[x, 16:32, cols] = both_parts
         return c
 
     lax.fori_loop(0, X, spread, 0)
 
     puts = []
     for i in range(PAIRS):
+        pair = slice(256 * i, 256 * (i + 1))
+
         def plane(x, c):
-            al = alpha_of(relax_ref[pl.ds(x, 1), 256 * i:256 * (i + 1)], wall_ref[pl.ds(x, 1), 256 * i:256 * (i + 1)])
-            val = jnp.dot(lt[...], rhs[x, :, 256 * i:256 * (i + 1)], preferred_element_type=F32) + al * a_ref[x + 2, :, 256 * i:256 * (i + 1)]
+            val = jnp.dot(lt[...], rhs[x, :, pair], preferred_element_type=F32) + a_ref[x + 2, :, pair]
             obuf[2 * i, pl.ds(x, LV, stride=X), :] = val[:, 0:128]
             obuf[2 * i + 1, pl.ds(x, LV, stride=X), :] = val[:, 128:256]
             return c
@@ -688,14 +724,14 @@
     smem = pl.BlockSpec(memory_space=pltpu.SMEM)
     dma = pltpu.SemaphoreType.DMA
     sds = jax.ShapeDtypeStruct
-    a, g1, g2, mac, norm = pl.pallas_call(
+    a, g2, mac, norm = pl.pallas_call(
         exchange,
         out_shape=(
-            pltpu.VMEM((X + 4, LV, CELLS), F32), pltpu.VMEM((8 * EXT, CELLS), F32), pltpu.VMEM((64, CELLS), F32),
+            pltpu.VMEM((X + 4, LV, CELLS), F32), pltpu.VMEM((64, CELLS), F32),
             pltpu.VMEM((MOM, X, 32), F32), pltpu.VMEM((2, 8, 128), F32),
         ),
         in_specs=[hbm] + [vmem] * 9,
-        out_specs=(vmem,) * 5,
+        out_specs=(vmem,) * 4,
         scratch_shapes=[
             pltpu.VMEM((LT, LV * X, 128), F32),
             pltpu.VMEM((X + 2, LV, CELLS), F32),
@@ -723,14 +759,19 @@
             pltpu.VMEM((2, CH, 128), F32),
             pltpu.VMEM((2, 2 * CH, CELLS), F32),
             pltpu.VMEM((26 * X, CELLS), F32),
-            pltpu.VMEM((64, CELLS), F32),
-            pltpu.VMEM((64, CELLS), F32),
+            pltpu.VMEM((2, 32, CELLS), F32),
             pltpu.VMEM((32, CELLS), F32),
             pltpu.VMEM((32, CELLS), F32),
             pltpu.VMEM((32, CELLS), F32),
+            pltpu.VMEM((2, 16, CELLS), F32),
+            pltpu.VMEM((16, CELLS), F32),
+            pltpu.VMEM((16, CELLS), F32),
             pltpu.VMEM((2, 4, 32, CELLS), F32),
             pltpu.VMEM((4, EXT, CELLS), F32),
+            pltpu.VMEM((8 * EXT, CELLS), F32),
             pltpu.VMEM((256, CELLS), F32),
+            pltpu.VMEM((56, LV), F32),
+            pltpu.VMEM((LV, 224), BF16),
             pltpu.VMEM((X * MOM, CELLS), F32),
             pltpu.VMEM((22 * X, CELLS), F32),
             pltpu.VMEM((2, 8, 128), F32),
@@ -741,7 +782,7 @@
             pltpu.VMEM((2, LV // 2, CELLS), F32),
             pltpu.VMEM((2, LV, CELLS), F32),
             dma((LT,)), dma((14,)), dma((14,)), dma((2,)), dma((2,)), dma((2,)), dma((2,)), dma((2,)), dma((2,)),
-            dma((3,)), dma((3,)), dma((4,)), dma((4,)),
+            dma((3,)), dma((3,)), dma((5,)), dma((5,)),
         ],
         compiler_params=pltpu.CompilerParams(collective_id=0, has_side_effects=True, vmem_limit_bytes=54 * 2 ** 20),
         name="exchange",
@@ -750,19 +791,18 @@
     out, mac, norm = pl.pallas_call(
         renew,
         out_shape=(sds((LV * X, CELLS), F32), sds((MOM, X, 32), F32), sds((2,), F32)),
-        in_specs=[vmem] * 8,
+        in_specs=[vmem] * 5,
         out_specs=(hbm, vmem, smem),
         scratch_shapes=[
             pltpu.VMEM((LT, LV * X, 128), F32),
-            pltpu.VMEM((LT, 512, 128), F32),
-            pltpu.VMEM((X, 256, CELLS), BF16),
-            pltpu.VMEM((LV, 256), BF16),
-            pltpu.VMEM((64, LV), F32),
+            pltpu.VMEM((LT, 64, 128), F32),
+            pltpu.VMEM((X, 32, CELLS), BF16),
+            pltpu.VMEM((LV, 32), BF16),
             dma((LT,)),
         ],
         compiler_params=pltpu.CompilerParams(vmem_limit_bytes=32 * 2 ** 20),
         name="renew",
-    )(a, g1, g2, relax, wall_mask, vel_index, mac, norm)
+    )(a, g2, vel_index, mac, norm)
     return (out.reshape(LV, X, CELLS), mac, norm)
 
 

time: 74.7 us -> 70.7 us (0.946)
  Pallas kernels: 73.9 us -> 69.9 us
    pallas_call x1, Pallas kernels: 9.31 us -> 7.04 us  [shards(): pl.pallas_call(renew, out_shape=(sds((LV * X, CELLS), F32), sds((MOM, X,...]
    pallas_call x1, Pallas kernels: 64.6 us -> 62.8 us  [shards(): pl.pallas_call(exchange, out_shape=(pltpu.VMEM((X + 4, LV, CELLS), F32),...]
where the time goes in v5:
time: 70.7 us; the launch traced here: 70.5 us
  Pallas kernels  69.9 us (99%)
    pallas_call x1, Pallas kernels, shards(): pl.pallas_call(exchange, out_shape=(pltpu.VMEM((X + 4, LV, CELLS), F32),...  62.8 us
    pallas_call x1, Pallas kernels, shards(): pl.pallas_call(renew, out_shape=(sds((LV * X, CELLS), F32), sds((MOM, X,...  7.04 us

profile of v5, /device:TPU:1, one launch (start us, length us, event | category | flops | bytes accessed | tf_op | source)
XLA Modules:
  0.0 70.5 jit_solution(17795960069850970090)
XLA Ops:
  0.6 0.0 copy-start
  0.6 62.8 %exchange.1 = (f32[12,128,1024]{2,1,0:T(8,128)S(1)}, f32[64,1024]{1,0:T(8,128)S(1)}, f32[13,8,32]{2,1,0:T(8,128)S(1)}, f32[2,8,128]{2,1,0:T(8,128)S(1)}) custom-call(f32[1024,1024]{1,0:T(8,128)} %bitcast.2, f32[8,1024]{1,0:T(8,128)} %relax_ref.1, s32[8,1024]{1,0:T(8,128)} %wall_ref.1, s32[3,128]{1,0:T(4,128)} %vel_ref.3, f32[13,13]{1,0:T(8,128)} %inv_ref.1, ...), custom_call_target="tpu_custom_call" | custom-call | tf_op jit(solution)/shard_map/exchange/pallas_call | solution.py:727
  63.5 0.0 copy-done
  63.5 7.0 %renew.1 = (f32[1024,1024]{1,0:T(8,128)}, f32[13,8,32]{2,1,0:T(8,128)}, f32[2]{0:T(128)}) custom-call(f32[12,128,1024]{2,1,0:T(8,128)S(1)} %get-tuple-element.10.a_ref, f32[64,1024]{1,0:T(8,128)S(1)} %get-tuple-element.11.g2_ref, s32[3,128]{1,0:T(4,128)S(1)} %copy-done, f32[13,8,32]{2,1,0:T(8,128)S(1)} %get-tuple-element.12.mac_ref, ...), custom_call_target="tpu_custom_call" | custom-call | tf_op jit(solution)/shard_map/renew/pallas_call | solution.py:791
Async XLA Ops:
  0.6 62.9 %copy-start = (s32[3,128]{1,0:T(4,128)S(1)}, s32[3,128]{1,0:T(4,128)}, u32[]{:S(2)}) copy-start(s32[3,128]{1,0:T(4,128)} %vel_ref.3) | copy-start | bytes 4612

commit v6 on v5

--- a/solution.py
+++ b/solution.py
@@ -413,6 +413,7 @@
         c = slice(128 * i, 128 * (i + 1))
         aa[0, :, c] = to_lower * at_[1, :, c]
         aa[X + 3, :, c] = to_upper * at_[X + 2, :, c]
+    send_total(0)
     settle(outer2)
     mine[1, 0] += from_left[16:32, :]
     mine[1, 1] += from_left[32:48, :]
@@ -420,7 +421,6 @@
     mine[1, X - 2] += from_right[32:48, :]
     pack(1)
     send_parts(1)
-    send_total(0)
 
     core = lax.rem(s, 2)
     mate = (v, s + 1 - 2 * core)
@@ -447,7 +447,7 @@
     give.wait()
     cout[...] = aa[out_end, mine_v, :] + cin[...]
     over_0 = hand(2, cout.at[0], cfar.at[0], over)
-    lax.fori_loop(3, 6, inner_third, 0)
+    lax.fori_loop(3, 7, inner_third, 0)
 
     all_totals(0)
     l1[...] = jnp.dot(kx[...], fbuf[0, 0:104, :], precision=HIGHEST, preferred_element_type=F32)
@@ -456,7 +456,7 @@
         h_out[1, HALO * k:HALO * (k + 1), :] = l1[8 * k + X - HALO:8 * k + X, :]
     halo2 = swap(3, h_out.at[1], h_left, h_out.at[0], h_right)
     own_sum(1)
-    lax.fori_loop(6, X + 1, inner_third, 0)
+    lax.fori_loop(7, X + 1, inner_third, 0)
     send_total(1)
     over_1 = hand(3, cout.at[1], cfar.at[1], over)
     settle(halo2)

time: 70.7 us -> 67.8 us (0.959)
  Pallas kernels: 69.9 us -> 67 us
    pallas_call x1, Pallas kernels: 62.8 us -> 60 us  [shards(): pl.pallas_call(exchange, out_shape=(pltpu.VMEM((X + 4, LV, CELLS), F32),...]
where the time goes in v6:
time: 67.8 us; the launch traced here: 67.7 us
  Pallas kernels  67 us (99%)
    pallas_call x1, Pallas kernels, shards(): pl.pallas_call(exchange, out_shape=(pltpu.VMEM((X + 4, LV, CELLS), F32),...  60 us
    pallas_call x1, Pallas kernels, shards(): pl.pallas_call(renew, out_shape=(sds((LV * X, CELLS), F32), sds((MOM, X,...  7.04 us

profile of v6, /device:TPU:1, one launch (start us, length us, event | category | flops | bytes accessed | tf_op | source)
XLA Modules:
  0.0 67.7 jit_solution(18017473473410382110)
XLA Ops:
  0.6 0.0 copy-start
  0.6 60.0 %exchange.1 = (f32[12,128,1024]{2,1,0:T(8,128)S(1)}, f32[64,1024]{1,0:T(8,128)S(1)}, f32[13,8,32]{2,1,0:T(8,128)S(1)}, f32[2,8,128]{2,1,0:T(8,128)S(1)}) custom-call(f32[1024,1024]{1,0:T(8,128)} %bitcast.2, f32[8,1024]{1,0:T(8,128)} %relax_ref.1, s32[8,1024]{1,0:T(8,128)} %wall_ref.1, s32[3,128]{1,0:T(4,128)} %vel_ref.3, f32[13,13]{1,0:T(8,128)} %inv_ref.1, ...), custom_call_target="tpu_custom_call" | custom-call | tf_op jit(solution)/shard_map/exchange/pallas_call | solution.py:727
  60.6 0.0 copy-done
  60.6 7.0 %renew.1 = (f32[1024,1024]{1,0:T(8,128)}, f32[13,8,32]{2,1,0:T(8,128)}, f32[2]{0:T(128)}) custom-call(f32[12,128,1024]{2,1,0:T(8,128)S(1)} %get-tuple-element.10.a_ref, f32[64,1024]{1,0:T(8,128)S(1)} %get-tuple-element.11.g2_ref, s32[3,128]{1,0:T(4,128)S(1)} %copy-done, f32[13,8,32]{2,1,0:T(8,128)S(1)} %get-tuple-element.12.mac_ref, ...), custom_call_target="tpu_custom_call" | custom-call | tf_op jit(solution)/shard_map/renew/pallas_call | solution.py:791
Async XLA Ops:
  0.6 60.0 %copy-start = (s32[3,128]{1,0:T(4,128)S(1)}, s32[3,128]{1,0:T(4,128)}, u32[]{:S(2)}) copy-start(s32[3,128]{1,0:T(4,128)} %vel_ref.3) | copy-start | bytes 4612

commit v7 on v6

--- a/solution.py
+++ b/solution.py
@@ -450,12 +450,13 @@
     lax.fori_loop(3, 7, inner_third, 0)
 
     all_totals(0)
-    l1[...] = jnp.dot(kx[...], fbuf[0, 0:104, :], precision=HIGHEST, preferred_element_type=F32)
+    l1[0:64, :] = jnp.dot(kx[0:64, :], fbuf[0, 0:104, :], precision=HIGHEST, preferred_element_type=F32)
     for k in range(8):
         h_out[0, HALO * k:HALO * (k + 1), :] = l1[8 * k:8 * k + HALO, :]
         h_out[1, HALO * k:HALO * (k + 1), :] = l1[8 * k + X - HALO:8 * k + X, :]
     halo2 = swap(3, h_out.at[1], h_left, h_out.at[0], h_right)
     own_sum(1)
+    l1[64:168, :] = jnp.dot(kx[64:168, :], fbuf[0, 0:104, :], precision=HIGHEST, preferred_element_type=F32)
     lax.fori_loop(7, X + 1, inner_third, 0)
     send_total(1)
     over_1 = hand(3, cout.at[1], cfar.at[1], over)
@@ -561,7 +562,6 @@
             dhl[x, 112:224, cols] = both_parts
         return c
 
-    lax.fori_loop(0, X, spread, 0)
     over_0.wait()
     over_1.wait()
     share = hand(4, cfar, cboth, mate)
@@ -581,7 +581,28 @@
         combine(x)
         return c
 
+    lax.fori_loop(0, X, spread, 0)
     lax.fori_loop(2, X - 2, middle, 0)
+    near.wait()
+    share.wait()
+    is_upper = (core == 0).astype(F32)
+    from_far = 2 + (X - 2) * core
+    from_near = 2 + (X - 2) * (1 - core)
+
+    def add_ends(i, carry):
+        for t in range(LT):
+            c = slice(128 * t, 128 * (t + 1))
+            aa[from_near + i, :, c] += cnear[i, :, c]
+            aa[from_far + i, mine_v, c] += jnp.where(wanted_of(mine_v) > 0, cfar[i, :, c], 0.0)
+            aa[from_far + i, mate_v, c] += jnp.where(wanted_of(mate_v) > 0, cboth[i, :, c], 0.0)
+        return carry
+
+    def wanted_of(rows):
+        towards = ct[1, rows, :]
+        return jnp.where(towards > 0, is_upper, 1.0 - is_upper)
+
+    lax.fori_loop(0, 2, add_ends, 0)
+
     settle(halo3)
     for k in range(4):
         fill(k, b2l[4 * k:4 * k + 4, :], b2out[8 * k:8 * k + 8, :], b2r[4 * k:4 * k + 4, :])
@@ -622,26 +643,6 @@
         else:
             f = l2[136 + 8 * (r - 5):144 + 8 * (r - 5), tile]
         mac_out[r] = pltpu.roll(f, turn, 1)[:, 0:32]
-
-    near.wait()
-    share.wait()
-    is_upper = (core == 0).astype(F32)
-    from_far = 2 + (X - 2) * core
-    from_near = 2 + (X - 2) * (1 - core)
-
-    def add_ends(i, carry):
-        for t in range(LT):
-            c = slice(128 * t, 128 * (t + 1))
-            aa[from_near + i, :, c] += cnear[i, :, c]
-            aa[from_far + i, mine_v, c] += jnp.where(wanted_of(mine_v) > 0, cfar[i, :, c], 0.0)
-            aa[from_far + i, mate_v, c] += jnp.where(wanted_of(mate_v) > 0, cboth[i, :, c], 0.0)
-        return carry
-
-    def wanted_of(rows):
-        towards = ct[1, rows, :]
-        return jnp.where(towards > 0, is_upper, 1.0 - is_upper)
-
-    lax.fori_loop(0, 2, add_ends, 0)
 
     def outside(j, c):
         combine(lax.rem(j + X - 2, X))

time: 67.8 us -> 67.8 us (level)
  no operation moved by 1% of the time
where the time goes in v7:
time: 67.8 us; the launch traced here: 67.7 us
  Pallas kernels  67 us (99%)
    pallas_call x1, Pallas kernels, shards(): pl.pallas_call(exchange, out_shape=(pltpu.VMEM((X + 4, LV, CELLS), F32),...  60 us
    pallas_call x1, Pallas kernels, shards(): pl.pallas_call(renew, out_shape=(sds((LV * X, CELLS), F32), sds((MOM, X,...  7.04 us

profile of v7, /device:TPU:1, one launch (start us, length us, event | category | flops | bytes accessed | tf_op | source)
XLA Modules:
  0.0 67.7 jit_solution(15980790664654668511)
XLA Ops:
  0.6 0.0 copy-start
  0.6 60.0 %exchange.1 = (f32[12,128,1024]{2,1,0:T(8,128)S(1)}, f32[64,1024]{1,0:T(8,128)S(1)}, f32[13,8,32]{2,1,0:T(8,128)S(1)}, f32[2,8,128]{2,1,0:T(8,128)S(1)}) custom-call(f32[1024,1024]{1,0:T(8,128)} %bitcast.2, f32[8,1024]{1,0:T(8,128)} %relax_ref.1, s32[8,1024]{1,0:T(8,128)} %wall_ref.1, s32[3,128]{1,0:T(4,128)} %vel_ref.3, f32[13,13]{1,0:T(8,128)} %inv_ref.1, ...), custom_call_target="tpu_custom_call" | custom-call | tf_op jit(solution)/shard_map/exchange/pallas_call | solution.py:728
  60.6 0.0 copy-done
  60.6 7.0 %renew.1 = (f32[1024,1024]{1,0:T(8,128)}, f32[13,8,32]{2,1,0:T(8,128)}, f32[2]{0:T(128)}) custom-call(f32[12,128,1024]{2,1,0:T(8,128)S(1)} %get-tuple-element.10.a_ref, f32[64,1024]{1,0:T(8,128)S(1)} %get-tuple-element.11.g2_ref, s32[3,128]{1,0:T(4,128)S(1)} %copy-done, f32[13,8,32]{2,1,0:T(8,128)S(1)} %get-tuple-element.12.mac_ref, ...), custom_call_target="tpu_custom_call" | custom-call | tf_op jit(solution)/shard_map/renew/pallas_call | solution.py:792
Async XLA Ops:
  0.6 60.0 %copy-start = (s32[3,128]{1,0:T(4,128)S(1)}, s32[3,128]{1,0:T(4,128)}, u32[]{:S(2)}) copy-start(s32[3,128]{1,0:T(4,128)} %vel_ref.3) | copy-start | bytes 4612

commit v8 on v7

--- a/solution.py
+++ b/solution.py
@@ -275,11 +275,11 @@
 
     lax.fori_loop(0, X, first, 0)
     pl.semaphore_wait(barrier, PEERS - 1 + 1 + 3)
-    halo = swap(0, rw, rwl, rw, rwr)
     edges[0, 0:16, :] = q1[1, 32:48, :]
     edges[1, 0:16, :] = q1[X, 16:32, :]
     outer1 = swap(1, edges.at[1, pl.ds(0, 16)], from_left.at[pl.ds(0, 16)],
                   edges.at[0, pl.ds(0, 16)], from_right.at[pl.ds(0, 16)])
+    halo = swap(0, rw, rwl, rw, rwr)
 
     def sum_first(x, c):
         mine[0, x] = stencil_moments(q1, x + 1)
@@ -396,13 +396,13 @@
     edges[1, 32:48, :] = q2[X + 1, 16:32, :]
     outer2 = swap(2, edges.at[1, pl.ds(16, 32)], from_left.at[pl.ds(16, 32)],
                   edges.at[0, pl.ds(16, 32)], from_right.at[pl.ds(16, 32)])
-    own_sum(0)
 
     def sum_second(x, c):
         mine[1, x] = stencil_moments(q2, x + 1)
         return c
 
     lax.fori_loop(0, X, sum_second, 0)
+    own_sum(0)
 
     def edge_third(j, c):
         third((X + 1) * j)
@@ -413,13 +413,13 @@
         c = slice(128 * i, 128 * (i + 1))
         aa[0, :, c] = to_lower * at_[1, :, c]
         aa[X + 3, :, c] = to_upper * at_[X + 2, :, c]
-    send_total(0)
     settle(outer2)
     mine[1, 0] += from_left[16:32, :]
     mine[1, 1] += from_left[32:48, :]
     mine[1, X - 1] += from_right[16:32, :]
     mine[1, X - 2] += from_right[32:48, :]
     pack(1)
+    send_total(0)
     send_parts(1)
 
     core = lax.rem(s, 2)

time: 67.8 us -> 66.6 us (0.982)
  Pallas kernels: 67 us -> 65.2 us
    pallas_call x1, Pallas kernels: 60 us -> 58.1 us  [shards(): pl.pallas_call(exchange, out_shape=(pltpu.VMEM((X + 4, LV, CELLS), F32),...]
where the time goes in v8:
time: 66.6 us; the launch traced here: 65.8 us
  Pallas kernels  65.2 us (98%)
    pallas_call x1, Pallas kernels, shards(): pl.pallas_call(exchange, out_shape=(pltpu.VMEM((X + 4, LV, CELLS), F32),...  58.1 us
    pallas_call x1, Pallas kernels, shards(): pl.pallas_call(renew, out_shape=(sds((LV * X, CELLS), F32), sds((MOM, X,...  7.04 us

profile of v8, /device:TPU:1, one launch (start us, length us, event | category | flops | bytes accessed | tf_op | source)
XLA Modules:
  0.0 65.8 jit_solution(612373756308233392)
XLA Ops:
  0.6 0.0 copy-start
  0.6 58.1 %exchange.1 = (f32[12,128,1024]{2,1,0:T(8,128)S(1)}, f32[64,1024]{1,0:T(8,128)S(1)}, f32[13,8,32]{2,1,0:T(8,128)S(1)}, f32[2,8,128]{2,1,0:T(8,128)S(1)}) custom-call(f32[1024,1024]{1,0:T(8,128)} %bitcast.2, f32[8,1024]{1,0:T(8,128)} %relax_ref.1, s32[8,1024]{1,0:T(8,128)} %wall_ref.1, s32[3,128]{1,0:T(4,128)} %vel_ref.3, f32[13,13]{1,0:T(8,128)} %inv_ref.1, ...), custom_call_target="tpu_custom_call" | custom-call | tf_op jit(solution)/shard_map/exchange/pallas_call | solution.py:728
  58.8 0.0 copy-done
  58.8 7.0 %renew.1 = (f32[1024,1024]{1,0:T(8,128)}, f32[13,8,32]{2,1,0:T(8,128)}, f32[2]{0:T(128)}) custom-call(f32[12,128,1024]{2,1,0:T(8,128)S(1)} %get-tuple-element.10.a_ref, f32[64,1024]{1,0:T(8,128)S(1)} %get-tuple-element.11.g2_ref, s32[3,128]{1,0:T(4,128)S(1)} %copy-done, f32[13,8,32]{2,1,0:T(8,128)S(1)} %get-tuple-element.12.mac_ref, ...), custom_call_target="tpu_custom_call" | custom-call | tf_op jit(solution)/shard_map/renew/pallas_call | solution.py:792
Async XLA Ops:
  0.6 58.2 %copy-start = (s32[3,128]{1,0:T(4,128)S(1)}, s32[3,128]{1,0:T(4,128)}, u32[]{:S(2)}) copy-start(s32[3,128]{1,0:T(4,128)} %vel_ref.3) | copy-start | bytes 4612

commit v9 on v8

--- a/solution.py
+++ b/solution.py
@@ -447,7 +447,7 @@
     give.wait()
     cout[...] = aa[out_end, mine_v, :] + cin[...]
     over_0 = hand(2, cout.at[0], cfar.at[0], over)
-    lax.fori_loop(3, 7, inner_third, 0)
+    lax.fori_loop(3, 8, inner_third, 0)
 
     all_totals(0)
     l1[0:64, :] = jnp.dot(kx[0:64, :], fbuf[0, 0:104, :], precision=HIGHEST, preferred_element_type=F32)
@@ -457,7 +457,7 @@
     halo2 = swap(3, h_out.at[1], h_left, h_out.at[0], h_right)
     own_sum(1)
     l1[64:168, :] = jnp.dot(kx[64:168, :], fbuf[0, 0:104, :], precision=HIGHEST, preferred_element_type=F32)
-    lax.fori_loop(7, X + 1, inner_third, 0)
+    lax.fori_loop(8, X + 1, inner_third, 0)
     send_total(1)
     over_1 = hand(3, cout.at[1], cfar.at[1], over)
     settle(halo2)

time: 66.6 us -> 66.6 us (level)
  no operation moved by 1% of the time
where the time goes in v9:
time: 66.6 us; the launch traced here: 65.7 us
  Pallas kernels  65.1 us (98%)
    pallas_call x1, Pallas kernels, shards(): pl.pallas_call(exchange, out_shape=(pltpu.VMEM((X + 4, LV, CELLS), F32),...  58.1 us
    pallas_call x1, Pallas kernels, shards(): pl.pallas_call(renew, out_shape=(sds((LV * X, CELLS), F32), sds((MOM, X,...  7.04 us

profile of v9, /device:TPU:1, one launch (start us, length us, event | category | flops | bytes accessed | tf_op | source)
XLA Modules:
  0.0 65.7 jit_solution(267906484729113679)
XLA Ops:
  0.6 0.0 copy-start
  0.6 58.1 %exchange.1 = (f32[12,128,1024]{2,1,0:T(8,128)S(1)}, f32[64,1024]{1,0:T(8,128)S(1)}, f32[13,8,32]{2,1,0:T(8,128)S(1)}, f32[2,8,128]{2,1,0:T(8,128)S(1)}) custom-call(f32[1024,1024]{1,0:T(8,128)} %bitcast.2, f32[8,1024]{1,0:T(8,128)} %relax_ref.1, s32[8,1024]{1,0:T(8,128)} %wall_ref.1, s32[3,128]{1,0:T(4,128)} %vel_ref.3, f32[13,13]{1,0:T(8,128)} %inv_ref.1, ...), custom_call_target="tpu_custom_call" | custom-call | tf_op jit(solution)/shard_map/exchange/pallas_call | solution.py:728
  58.7 0.0 copy-done
  58.7 7.0 %renew.1 = (f32[1024,1024]{1,0:T(8,128)}, f32[13,8,32]{2,1,0:T(8,128)}, f32[2]{0:T(128)}) custom-call(f32[12,128,1024]{2,1,0:T(8,128)S(1)} %get-tuple-element.10.a_ref, f32[64,1024]{1,0:T(8,128)S(1)} %get-tuple-element.11.g2_ref, s32[3,128]{1,0:T(4,128)S(1)} %copy-done, f32[13,8,32]{2,1,0:T(8,128)S(1)} %get-tuple-element.12.mac_ref, ...), custom_call_target="tpu_custom_call" | custom-call | tf_op jit(solution)/shard_map/renew/pallas_call | solution.py:792
Async XLA Ops:
  0.6 58.1 %copy-start = (s32[3,128]{1,0:T(4,128)S(1)}, s32[3,128]{1,0:T(4,128)}, u32[]{:S(2)}) copy-start(s32[3,128]{1,0:T(4,128)} %vel_ref.3) | copy-start | bytes 4612
